TPU v7x, 512 devices: a whole 4x4x16 slice. The times are simulated.
512 devices in a mesh: pulse: 128 (over x, z, core), chan: 4 (over y).
Axes of the slice: x: 4, y: 4, z: 16, core: 2. Of those that a mesh axis runs over, the one named last changes fastest.
Arguments:
- echoes: bfloat16 [16, 512, 2, 8192], P('chan', 'pulse'), may hold values from -6 to 6
- replica: bfloat16 [2, 4096], replicated, may hold values from -0.0625 to 0.0625
- recon_filters: bfloat16 [16, 16, 2, 64], replicated, may hold values from -0.125 to 0.125
- span_offset: int32 [1024], P('pulse'), may hold values from 0 to 4
- span_width: int32 [1024], P('pulse'), may hold values from 1 to 4
- aperture_edges: int32 [2, 1024], P(None, 'pulse'), may hold values from 0 to 64
Outputs:
- image: bfloat16 [16, 2, 1024, 512], P(None, None, 'pulse', 'chan')
All inputs are finite; a program needn't handle non-finite values.
Results may differ from a plain program's by a relative error of at most 0.012.
Values may be sent and summed in bfloat16 or wider, within the bound.
No kernel may reach another device: no remote copies, remote signals or barrier semaphores. Data moves between devices by JAX's collectives and lax.ppermute only.
A program may use at most 64 MiB of HBM per device.

v0:
```python
import math

import jax
import jax.numpy as jnp
from jax import lax
from jax.sharding import PartitionSpec as P

MIG = 4
WMAX = 4


def passed_along(array, axis, by):
    count = lax.axis_size(axis)
    pairs = [(i, i + by) for i in range(count) if 0 <= i + by < count]
    return lax.ppermute(array, axis, pairs)


def padded_2(cells, sides, width):
    for axis, dim in sides:
        count = lax.axis_size(axis)
        ends = count - 1
        head = lax.slice_in_dim(cells, 0, width, axis=dim)
        tail = lax.slice_in_dim(cells, cells.shape[dim] - width, cells.shape[dim], axis=dim)
        cells = jnp.concatenate(
            [
                lax.ppermute(tail, axis, [(i, (i + 1) % count) for i in range(ends)]),
                cells,
                lax.ppermute(head, axis, [((i + 1) % count, i) for i in range(ends)]),
            ],
            axis=dim,
        )
    return cells


def banded(taps_row, block_len, span_len):
    period = span_len + 4
    extended = jnp.concatenate([taps_row, jnp.zeros((period - taps_row.shape[0],), taps_row.dtype)])
    tiled = jnp.tile(extended, block_len)[: block_len * span_len]
    return tiled.reshape(block_len, span_len).T


def range_matrix(replica, block_len):
    tap_count = replica.shape[1]
    span_len = 4 * block_len + tap_count
    real_part = banded(replica[0], block_len, span_len)
    imag_part = banded(replica[1], block_len, span_len)
    from_real = jnp.stack([real_part, imag_part], 1)
    from_imag = jnp.stack([-imag_part, real_part], 1)
    matrix = jnp.stack([from_real, from_imag], 0)
    return matrix.reshape(2 * span_len, 2 * block_len)


def compress(echoes, replica):
    channels, pulses, _, samples = echoes.shape
    tap_count = replica.shape[1]
    bin_count = (samples - tap_count) // 4
    block_len = min(128, bin_count)
    span_len = 4 * block_len + tap_count
    block_total = bin_count // block_len
    group = math.gcd(block_total, 8)
    matrix = lax.optimization_barrier(range_matrix(replica, block_len))

    def one_group(group_id):
        windows = [
            lax.dynamic_slice_in_dim(
                echoes, (group_id * group + member) * 4 * block_len, span_len, 3
            )
            for member in range(group)
        ]
        window_rows = jnp.stack(windows, 0).reshape(group * channels * pulses, 2 * span_len)
        return jnp.dot(window_rows, matrix, preferred_element_type=jnp.float32).astype(jnp.bfloat16)

    blocks = lax.map(one_group, jnp.arange(block_total // group, dtype=jnp.int32))
    blocks = blocks.reshape(block_total, channels, pulses, 2, block_len)
    return blocks.transpose(1, 3, 0, 4, 2).reshape(channels, 2, bin_count, pulses)


def migrate(joined, span_offset, span_width):
    bin_count = span_offset.shape[0]
    columns = jnp.arange(joined.shape[2])
    span_first = jnp.arange(bin_count) + span_offset
    within = (columns[None, :] >= span_first[:, None]) & (
        columns[None, :] < (span_first + span_width)[:, None]
    )
    weight = within.astype(jnp.float32) / span_width[:, None].astype(jnp.float32)
    return jnp.einsum(
        "rs,cisp->cirp", weight, joined.astype(jnp.float32), precision=lax.Precision.HIGHEST
    )


def aperture(aperture_edges, pulse_first, pulse_count, all_pulses):
    global_pulse = pulse_first + jnp.arange(pulse_count)
    lower_edge = aperture_edges[0][:, None]
    upper_edge = aperture_edges[1][:, None]
    return (
        (global_pulse[None, :] >= lower_edge) & (global_pulse[None, :] < all_pulses - upper_edge)
    ).astype(jnp.float32)


def azimuth(padded, filters):
    channels, _, bin_count, padded_len = padded.shape
    subbands = filters.shape[0]
    tap_count = filters.shape[3]
    pulses = padded_len - tap_count
    span_len = tap_count + 4
    step_count = span_len // 4
    quartets = padded.reshape(channels, 2, bin_count, padded_len // 4, 4)
    window = jnp.stack(
        [
            quartets[:, :, :, shift_step : shift_step + pulses // 4, :]
            for shift_step in range(step_count)
        ],
        4,
    )
    window = window.transpose(2, 3, 0, 1, 4, 5).reshape(
        bin_count * (pulses // 4), channels * 2 * span_len
    )
    offset = jnp.arange(span_len)[:, None] - jnp.arange(4)[None, :]
    inside = (offset >= 0) & (offset < tap_count)
    tap_index = jnp.clip(offset, 0, tap_count - 1)
    picked = jnp.where(inside, jnp.take(filters, tap_index, axis=3), 0)
    real_part = picked[:, :, 0]
    imag_part = picked[:, :, 1]
    from_real = jnp.stack([real_part, imag_part], 3)
    from_imag = jnp.stack([-imag_part, real_part], 3)
    matrix = jnp.stack([from_real, from_imag], 2)
    matrix = matrix.transpose(1, 2, 3, 0, 4, 5).reshape(channels * 2 * span_len, subbands * 8)
    result = jnp.dot(window, matrix, preferred_element_type=jnp.float32)
    result = result.reshape(bin_count, pulses // 4, subbands, 2, 4).transpose(2, 3, 0, 1, 4)
    return result.reshape(subbands, 2, bin_count, pulses)


def body(echoes, replica, recon_filters, span_offset, span_width, aperture_edges):
    rim_len = MIG + WMAX - 1
    compressed = compress(echoes, replica)
    turned = lax.all_to_all(
        lax.all_to_all(compressed, "pulse", split_axis=2, concat_axis=3, tiled=True),
        "chan",
        split_axis=3,
        concat_axis=0,
        tiled=True,
    )
    pulse_first = lax.axis_index("chan") * turned.shape[3]
    all_pulses = turned.shape[3] * lax.axis_size("chan")
    rim_bins = passed_along(turned[:, :, :rim_len, :], "pulse", -1)
    joined = jnp.concatenate([turned, rim_bins], 2)
    migrated = migrate(joined, span_offset, span_width)
    keep_mask = aperture(aperture_edges, pulse_first, migrated.shape[3], all_pulses)
    corrected = (migrated * keep_mask[None, None]).astype(jnp.bfloat16)
    half_taps = recon_filters.shape[3] // 2
    padded = padded_2(corrected, (("chan", 3),), half_taps)
    image = azimuth(padded, recon_filters)
    return image.astype(jnp.bfloat16)


def solution(mesh):
    return jax.shard_map(
        body,
        mesh=mesh,
        in_specs=(
            P("chan", "pulse", None, None),
            P(),
            P(),
            P("pulse"),
            P("pulse"),
            P(None, "pulse"),
        ),
        out_specs=P(None, None, "pulse", "chan"),
        check_vma=False,
    )
```

profile of v0, /device:TPU:1, one launch (start us, length us, event | category | flops | bytes accessed | tf_op | source)
XLA Modules:
  0.0 184.4 jit_solution(16065123050115684101)
XLA Ops:
  0.0 0.9 slice_reduce_fusion
  1.0 2.1 %tile.21 = bf16[590336]{0:T(1024)(128)(2,1)S(1)} reshape(bf16[128,4612]{1,0:T(8,128)(2,1)S(1)} %tile.20) | data formatting | bytes 2361344 | tf_op jit(solution)/shard_map/tile | solution.py:38
  3.2 1.5 reshape.163
  4.7 0.7 copy.64
  5.4 1.2 fusion.5
  6.7 3.1 %tile.9 = bf16[590336]{0:T(1024)(128)(2,1)} reshape(bf16[128,4612]{1,0:T(8,128)(2,1)S(1)} %tile.8) | data formatting | bytes 2361344 | tf_op jit(solution)/shard_map/tile | solution.py:38
  9.8 1.3 slice-done
  11.1 1.3 reshape.162
  12.4 1.4 copy.63
  13.9 2.1 %maximum_bitcast_fusion = (bf16[1,4608,2,128]{3,1,2,0:T(8,128)(2,1)S(1)}, bf16[1,4608,2,128]{3,1,2,0:T(8,128)(2,1)S(1)}) fusion(bf16[4608,1,128]{2,0,1:T(8,128)(2,1)S(1)} %bitcast.196, bf16[4608,1,128]{2,0,1:T(8,128)(2,1)} %bitcast.202, bf16[4608,1,128]{2,0,1:T(8,128)(2,1)S(1)} %copy-done.2), kind=kLoop, calls=%fused_computation.5 | loop fusion | flops 2359296 | bytes 8257536 | tf_op jit(solution)/shard_map/stack | solution.py:49
  15.9 0.4 pad_maximum_fusion
  16.4 44.9 %copy.65 = bf16[2,4608,2,128]{3,2,1,0:T(2,128)(2,1)S(1)} copy(bf16[2,4608,2,128]{3,1,2,0:T(8,128)(2,1)S(1)} %pad_maximum_fusion) | data formatting | bytes 9437184 | tf_op jit(solution)/shard_map/stack | solution.py:49
  61.2 2.5 %copy.110 = bf16[1152,8,2,128]{3,1,2,0:T(8,128)(2,1)S(1)} copy(bf16[1152,8,2,128]{3,2,1,0:T(2,128)(2,1)S(1)} %bitcast.195) | data formatting | bytes 9437184
  65.7 0.3 copy.95
  66.0 0.8 convolution_convert_fusion
  66.9 2.5 %copy.91 = bf16[4,2,8,128,4]{4,1,0,3,2:T(2,128)(2,1)S(1)} copy(bf16[4,2,8,128,4]{3,2,4,1,0:T(8,128)(2,1)S(1)} %bitcast.211) | data formatting | bytes 131072 | tf_op jit(solution)/shard_map/reshape | solution.py:75
  69.4 4.5 %reshape.183 = bf16[128,2,128]{2,1,0:T(2,128)(2,1)} reshape(bf16[1024,4,2,4]{3,2,1,0:T(2,128)(2,1)S(1)} %bitcast.199) | data formatting | bytes 131072
  73.9 20.4 %all-to-all-start = ((bf16[128,2,128]{2,1,0:T(2,128)(2,1)}), bf16[128,2,128]{2,1,0:T(2,128)(2,1)S(1)}, u32[]{:S(2)}, u32[]{:S(2)}) async-start(bf16[128,2,128]{2,1,0:T(2,128)(2,1)} %reshape.183), calls=%async_computation | async-start | bytes 131072 | tf_op jit(solution)/shard_map/all_to_all | solution.py:137
  94.4 0.4 copy.77
  95.2 2.3 %gather_fusion = bf16[272,16,16,2]{2,1,3,0:T(8,128)(2,1)S(1)} fusion(bf16[16,16,2,64]{1,0,3,2:T(8,128)(2,1)S(1)} %copy.77, s32[1024]{0:T(1024)S(1)} %pad_clamp_fusion), kind=kCustom, calls=%fused_computation | custom fusion | bytes 558144 | tf_op jit(solution)/shard_map/jit(_take)/gather | solution.py:121
  97.5 0.9 select_bitcast_fusion
  98.4 1.7 slice_bitcast_fusion
  100.1 1.1 fusion.46
  101.3 8.0 %all-to-all-done = bf16[128,2,128]{2,1,0:T(2,128)(2,1)S(1)} async-done(((bf16[128,2,128]{2,1,0:T(2,128)(2,1)}), bf16[128,2,128]{2,1,0:T(2,128)(2,1)S(1)}, u32[]{:S(2)}, u32[]{:S(2)}) %all-to-all-start) | async-done | bytes 65568 | tf_op jit(solution)/shard_map/all_to_all | solution.py:137
  109.3 4.5 %reshape.184 = bf16[1024,4,2,4]{3,2,1,0:T(2,128)(2,1)S(1)} reshape(bf16[128,2,128]{2,1,0:T(2,128)(2,1)S(1)} %all-to-all-done) | data formatting | bytes 131072
  113.8 10.1 %copy.92 = bf16[4,2,128,8,4]{3,2,4,1,0:T(8,128)(2,1)} copy(bf16[4,2,128,8,4]{4,1,0,3,2:T(2,128)(2,1)S(1)} %bitcast.200) | data formatting | bytes 131072 | tf_op jit(solution)/shard_map/all_to_all | solution.py:137
  123.9 2.1 %copy.69 = bf16[4,2,8,128,4]{2,4,3,1,0:T(4,128)(2,1)S(1)} copy(bf16[4,2,8,128,4]{2,3,4,1,0:T(8,128)(2,1)} %bitcast.204) | data formatting | bytes 131072 | tf_op jit(solution)/shard_map/all_to_all | solution.py:137
  126.0 2.1 %copy.112 = bf16[4,2,8,512]{2,1,0,3:T(2,128)(2,1)} copy(bf16[4,2,8,512]{2,3,1,0:T(8,128)(2,1)S(1)} %bitcast.205) | data formatting | bytes 131072 | tf_op jit(solution)/shard_map/all_to_all | solution.py:137
  128.1 2.9 %reshape.185 = bf16[4,2,4096]{2,1,0:T(2,128)(2,1)} reshape(bf16[512,4,2,8]{3,2,1,0:T(2,128)(2,1)} %bitcast.206) | data formatting | bytes 131072
  131.0 4.2 %all-to-all-start.1 = ((bf16[4,2,4096]{2,1,0:T(2,128)(2,1)}), bf16[4,2,4096]{2,1,0:T(2,128)(2,1)S(1)}, u32[]{:S(2)}, u32[]{:S(2)}) async-start(bf16[4,2,4096]{2,1,0:T(2,128)(2,1)} %reshape.185), calls=%async_computation.1 | async-start | bytes 131072 | tf_op jit(solution)/shard_map/all_to_all | solution.py:136
  135.2 1.5 copy.78
  136.7 1.5 copy.79
  138.2 2.6 %copy.80 = bf16[16,16,68,1,4]{2,1,4,3,0:T(8,128)(2,1)S(1)} copy(bf16[16,16,68,1,4]{1,0,4,2,3:T(8,128)(2,1)} %fusion.46) | data formatting | bytes 278528 | tf_op jit(solution)/shard_map/neg | solution.py:125
  140.8 1.2 reshape.186
  142.0 1.3 copy.71
  143.3 3.6 %collective-permute-start = (bf16[16,2,7,128]{3,2,1,0:T(8,128)(2,1)S(1)}, bf16[16,2,7,128]{3,2,1,0:T(8,128)(2,1)S(1)}, u32[]{:S(2)}, u32[]{:S(2)}) collective-permute-start(bf16[16,2,7,128]{3,2,1,0:T(8,128)(2,1)S(1)} %bitcast.213), channel_id=1, source_target_pairs={{4,0},{8,4},{12,8},{16,12},{20,16},{24,20},{28,24},{32,28},{36,32}... | collective-permute-start | bytes 172040 | tf_op jit(solution)/shard_map/ppermute | solution.py:15
  147.1 2.0 %collective-permute-done = bf16[16,2,7,128]{3,2,1,0:T(8,128)(2,1)S(1)} collective-permute-done((bf16[16,2,7,128]{3,2,1,0:T(8,128)(2,1)S(1)}, bf16[16,2,7,128]{3,2,1,0:T(8,128)(2,1)S(1)}, u32[]{:S(2)}, u32[]{:S(2)}) %collective-permute-start) | collective-permute-done | bytes 57376 | tf_op jit(solution)/shard_map/ppermute | solution.py:15
  149.2 0.3 fusion.10
  149.5 3.6 %collective-permute-start.1 = (bf16[16,2,8,32]{3,2,1,0:T(8,128)(2,1)S(1)}, bf16[16,2,8,32]{3,2,1,0:T(8,128)(2,1)S(1)}, u32[]{:S(2)}, u32[]{:S(2)}) collective-permute-start(bf16[16,2,8,32]{3,2,1,0:T(8,128)(2,1)S(1)} %get-tuple-element.25), channel_id=1, source_target_pairs={{0,1},{1,2},{2,3},{4,5},{5,6},{6,7},{8,9},{9,10},{10,11},{12,13},{... | collective-permute-start | bytes 49160 | tf_op jit(solution)/shard_map/ppermute | solution.py:26
  153.2 1.5 collective-permute-start.2
  155.0 1.7 copy.84
  156.7 1.9 %reshape.168 = bf16[2176,128]{0,1:T(8,128)(2,1)S(1)} reshape(bf16[16,2,68,16,2,4]{2,1,0,5,4,3:T(2,128)(2,1)S(1)} %copy.84) | data formatting | bytes 1114112 | tf_op jit(solution)/shard_map/reshape | solution.py:127
  158.9 0.5 copy.73
  160.7 3.5 %copy-done.1 = bf16[16,2,8,32,17,4]{0,2,5,3,1,4:T(8,128)(2,1)} copy-done((bf16[16,2,8,32,17,4]{0,2,5,3,1,4:T(8,128)(2,1)}, bf16[16,2,8,32,17,4]{0,2,5,3,1,4:T(8,128)(2,1)S(1)}, u32[]{:S(2)}) %copy-start.1) | copy-done | bytes 1114136
  164.2 14.9 %copy.74 = bf16[8,32,16,2,17,4]{1,0,5,4,3,2:T(8,128)(2,1)} copy(bf16[8,32,16,2,17,4]{2,0,5,1,3,4:T(8,128)(2,1)} %bitcast.197) | data formatting | bytes 2228224 | tf_op jit(solution)/shard_map/transpose | solution.py:115
  179.1 3.0 %fusion.6 = bf16[16,2,8,32,4]{3,0,4,1,2:T(8,128)(2,1)S(1)} fusion(bf16[8,32,2176,1,1]{1,0,2,4,3:T(8,128)(2,1)} %bitcast.203, bf16[16,2,4,2176]{3,2,1,0:T(4,128)(2,1)S(1)} %dot_general.20), kind=kOutput, calls=%fused_computation.11 | convolution fusion | flops 142639104 | bytes 1736704 | tf_op jit(solution)/shard_map/dot_general | solution.py:128
  182.1 0.8 copy.87
  183.0 1.0 copy.88
  (68 shorter events, 4.6 us)
Async XLA Ops:
  9.8 1.3 slice-start
  12.4 1.4 copy-start.2
  61.2 2.6 %copy-start = (bf16[4,4,2,8192]{3,2,1,0:T(2,128)(2,1)S(1)}, bf16[4,4,2,8192]{3,2,1,0:T(2,128)(2,1)}, u32[]{:S(2)}) copy-start(bf16[4,4,2,8192]{3,2,1,0:T(2,128)(2,1)} %param.6) | copy-start | bytes 1572868
  66.8 27.6 %copy-start.5 = (s32[2,8]{1,0:T(2,128)S(1)}, s32[2,8]{1,0:T(2,128)}, u32[]{:S(2)}) copy-start(s32[2,8]{1,0:T(2,128)} %param.11) | copy-start | bytes 196
  66.8 27.6 %copy-start.4 = (bf16[16,16,2,64]{3,2,1,0:T(2,128)(2,1)S(1)}, bf16[16,16,2,64]{3,2,1,0:T(2,128)(2,1)}, u32[]{:S(2)}) copy-start(bf16[16,16,2,64]{3,2,1,0:T(2,128)(2,1)} %param.8) | copy-start | bytes 196612
  73.9 35.4 %all-to-all-start = ((bf16[128,2,128]{2,1,0:T(2,128)(2,1)}), bf16[128,2,128]{2,1,0:T(2,128)(2,1)S(1)}, u32[]{:S(2)}, u32[]{:S(2)}) async-start(bf16[128,2,128]{2,1,0:T(2,128)(2,1)} %reshape.183), calls=%async_computation | async-start | bytes 131072 | tf_op jit(solution)/shard_map/all_to_all | solution.py:137
  123.9 11.3 %copy-start.6 = (s32[8]{0:T(128)S(1)}, s32[8]{0:T(128)}, u32[]{:S(2)}) copy-start(s32[8]{0:T(128)} %param.9) | copy-start | bytes 100
  123.9 11.3 %copy-start.7 = (s32[8]{0:T(128)S(1)}, s32[8]{0:T(128)}, u32[]{:S(2)}) copy-start(s32[8]{0:T(128)} %param.10) | copy-start | bytes 100
  123.9 11.3 %copy-start.3 = (bf16[16,16,68,1,4]{1,0,4,2,3:T(8,128)(2,1)S(1)}, bf16[16,16,68,1,4]{1,0,4,2,3:T(8,128)(2,1)}, u32[]{:S(2)}) copy-start(bf16[16,16,68,1,4]{1,0,4,2,3:T(8,128)(2,1)} %get-tuple-element.20) | copy-start | bytes 417796
  131.0 9.8 %all-to-all-start.1 = ((bf16[4,2,4096]{2,1,0:T(2,128)(2,1)}), bf16[4,2,4096]{2,1,0:T(2,128)(2,1)S(1)}, u32[]{:S(2)}, u32[]{:S(2)}) async-start(bf16[4,2,4096]{2,1,0:T(2,128)(2,1)} %reshape.185), calls=%async_computation.1 | async-start | bytes 131072 | tf_op jit(solution)/shard_map/all_to_all | solution.py:136
  143.3 5.8 %collective-permute-start = (bf16[16,2,7,128]{3,2,1,0:T(8,128)(2,1)S(1)}, bf16[16,2,7,128]{3,2,1,0:T(8,128)(2,1)S(1)}, u32[]{:S(2)}, u32[]{:S(2)}) collective-permute-start(bf16[16,2,7,128]{3,2,1,0:T(8,128)(2,1)S(1)} %bitcast.213), channel_id=1, source_target_pairs={{4,0},{8,4},{12,8},{16,12},{20,16},{24,20},{28,24},{32,28},{36,32}... | collective-permute-start | bytes 172040 | tf_op jit(solution)/shard_map/ppermute | solution.py:15
  149.5 9.2 %collective-permute-start.1 = (bf16[16,2,8,32]{3,2,1,0:T(8,128)(2,1)S(1)}, bf16[16,2,8,32]{3,2,1,0:T(8,128)(2,1)S(1)}, u32[]{:S(2)}, u32[]{:S(2)}) collective-permute-start(bf16[16,2,8,32]{3,2,1,0:T(8,128)(2,1)S(1)} %get-tuple-element.25), channel_id=1, source_target_pairs={{0,1},{1,2},{2,3},{4,5},{5,6},{6,7},{8,9},{9,10},{10,11},{12,13},{... | collective-permute-start | bytes 49160 | tf_op jit(solution)/shard_map/ppermute | solution.py:26
  153.2 5.6 %collective-permute-start.2 = (bf16[16,2,8,32]{3,2,1,0:T(8,128)(2,1)S(1)}, bf16[16,2,8,32]{3,2,1,0:T(8,128)(2,1)S(1)}, u32[]{:S(2)}, u32[]{:S(2)}) collective-permute-start(bf16[16,2,8,32]{3,2,1,0:T(8,128)(2,1)S(1)} %get-tuple-element.26), channel_id=1, source_target_pairs={{1,0},{2,1},{3,2},{5,4},{6,5},{7,6},{9,8},{10,9},{11,10},{13,12},{... | collective-permute-start | bytes 49160 | tf_op jit(solution)/shard_map/ppermute | solution.py:28
  160.7 3.5 %copy-start.1 = (bf16[16,2,8,32,17,4]{0,2,5,3,1,4:T(8,128)(2,1)}, bf16[16,2,8,32,17,4]{0,2,5,3,1,4:T(8,128)(2,1)S(1)}, u32[]{:S(2)}) copy-start(bf16[16,2,8,32,17,4]{0,2,5,3,1,4:T(8,128)(2,1)S(1)} %fusion.13) | copy-start | bytes 3342340
where the time goes:
time: 188 us; the launch traced here: 184 us
  local copies, waits for them, and re-layouts  130 us (69%)
  starting transfers between devices  33.3 us (18%)
  waiting for transfers between devices  10.1 us (5%)
  other arithmetic  6.3 us (3%)
  matrix products  4.09 us (2%)
    another operation x1, local copies, waits for them, and re-layouts, range_matrix(): matrix = jnp.stack([from_real, from_imag], 0)  44.9 us
    unnamed x46, local copies, waits for them, and re-layouts  22.6 us
    all_to_all x1, starting transfers between devices, body(): lax.all_to_all(compressed, 'pulse', split_axis=2, concat_axis=3, tiled=True)  20.4 us
    transpose x1, local copies, waits for them, and re-layouts, azimuth(): window.transpose(2, 3, 0, 1, 4, 5)  14.9 us
    all_to_all x3, local copies, waits for them, and re-layouts, body(): lax.all_to_all(compressed, 'pulse', split_axis=2, concat_axis=3, tiled=True)  14.3 us
    all_to_all x1, waiting for transfers between devices, body(): lax.all_to_all(compressed, 'pulse', split_axis=2, concat_axis=3, tiled=True)  8.02 us
    another operation x4, local copies, waits for them, and re-layouts, banded(): tiled = jnp.tile(extended, block_len)[:block_len * span_len]  5.39 us
    another operation x3, local copies, waits for them, and re-layouts, azimuth(): from_real = jnp.stack([real_part, imag_part], 3)  4.7 us
  transfers between devices with their start and end apart: 5, of which 2 were waited for; matrix products, arithmetic and copies ran while one was open for 9% of the time, Pallas kernels for 0%

commit v1 on v0

v1 whole, which is shorter than its diff:
```python
import functools

import jax
import jax.numpy as jnp
from jax import lax
from jax.experimental import pallas as pl
from jax.experimental.pallas import tpu as pltpu
from jax.sharding import PartitionSpec as P

F32 = jnp.float32
BF16 = jnp.bfloat16
LANES = 128
NT = (((1,), (1,)), ((), ()))


def lane_ids(rows):
    return lax.broadcasted_iota(jnp.int32, (rows, LANES), 1)


def swap_blocks(arrays, width):
    arrays = list(arrays)
    group = lane_ids(arrays[0].shape[0]) // width
    bit = 1
    while bit < len(arrays):
        low = (group & bit) == 0
        shift = bit * width
        for first in range(len(arrays)):
            if first & bit:
                continue
            second = first | bit
            a, b = arrays[first], arrays[second]
            arrays[first] = jnp.where(low, a, pltpu.roll(b, shift, 1))
            arrays[second] = jnp.where(low, pltpu.roll(a, LANES - shift, 1), b)
        bit *= 2
    return arrays


def compress_kernel(echo_ref, replica_ref, out_ref, taps, windows, parts, rows, chunks):
    lane = lane_ids(32)
    shift = 4 * lax.broadcasted_iota(jnp.int32, (32, LANES), 0)
    zero = jnp.zeros((32, LANES), F32)
    for part in range(2):
        previous = zero
        for m in range(33):
            if m < 32:
                row = replica_ref[part : part + 1, m * LANES : (m + 1) * LANES].astype(F32)
                rolled = pltpu.roll(
                    jnp.broadcast_to(row, (32, LANES)), 0, 1, stride=4, stride_axis=0
                )
            else:
                rolled = zero
            tile = jnp.where(lane >= shift, rolled, previous).astype(BF16)
            previous = rolled
            for a in range(4):
                taps[
                    part * 128 + 32 * a : part * 128 + 32 * a + 32,
                    (m + a) * LANES : (m + a + 1) * LANES,
                ] = tile
        for a in range(4):
            base = part * 128 + 32 * a
            if a:
                taps[base : base + 32, : a * LANES] = jnp.zeros((32, a * LANES), BF16)
            if a < 3:
                taps[base : base + 32, (33 + a) * LANES :] = jnp.zeros(
                    (32, (3 - a) * LANES), BF16
                )
    for part in range(2):
        for w in range(8):
            at = part * 128 + w * 16
            windows[at : at + 16, :] = echo_ref[part, :, 512 * w : 512 * w + 4608]
    product = lax.dot_general(taps[...], windows[...], NT, preferred_element_type=F32)
    parts[0:128, :] = product[:128, :128] - product[128:, 128:]
    parts[128:256, :] = product[:128, 128:] + product[128:, :128]
    pieces = [parts[pl.ds(128 * (g % 2) + g // 2, 32, stride=4), :] for g in range(8)]
    for w, piece in enumerate(swap_blocks(pieces, 16)):
        rows[32 * w : 32 * w + 32, :] = piece
    rows[256:264, :] = jnp.zeros((8, LANES), F32)
    for k in range(4):
        chunks[pl.ds(k, 128, stride=4), :] = rows[pl.ds(k, 128, stride=2), :]
    out_ref[...] = chunks[...].astype(BF16)


def compress(echo_rows, replica):
    return pl.pallas_call(
        compress_kernel,
        out_shape=jax.ShapeDtypeStruct((512, LANES), BF16),
        scratch_shapes=[
            pltpu.VMEM((256, 4608), BF16),
            pltpu.VMEM((256, 4608), BF16),
            pltpu.VMEM((256, LANES), F32),
            pltpu.VMEM((264, LANES), F32),
            pltpu.VMEM((512, LANES), F32),
        ],
        compiler_params=pltpu.CompilerParams(vmem_limit_bytes=24 << 20),
        cost_estimate=pl.CostEstimate(
            flops=2 * 256 * 256 * 4608, bytes_accessed=1 << 20, transcendentals=0
        ),
        name="compress",
    )(echo_rows, replica)


def migrate_kernel(turned_ref, info_ref, out_ref, quads, rows):
    quads[...] = turned_ref[...].astype(F32)
    quad = [quads[pl.ds(k, 128, stride=4), :] for k in range(4)]
    lane = lane_ids(128)
    group = lane // 32
    pulse = 4 * lax.broadcasted_iota(jnp.int32, (128, LANES), 0) + lane % 4
    shifted = [quad]
    for f in range(1, 4):
        rolled = [pltpu.roll(q, LANES - 32 * f, 1) for q in quad]
        shifted.append([jnp.where(group < 4 - f, rolled[k], rolled[k + 1]) for k in range(3)])
    rows[0:16, :] = jnp.zeros((16, LANES), F32)
    rows[272:288, :] = jnp.zeros((16, LANES), F32)
    for half in range(2):
        first = info_ref[half : half + 1, :]
        width = info_ref[2 + half : 3 + half, :]
        low = info_ref[4 + half : 5 + half, :]
        high = info_ref[6 + half : 7 + half, :]
        total = jnp.zeros((128, LANES), F32)
        for step in range(8):
            inside = (first <= step) & (step < first + width)
            total = total + jnp.where(inside, shifted[step % 4][half + step // 4], 0.0)
        total = total * (1.0 / width.astype(F32))
        keep = (pulse >= low) & (pulse < 512 - high)
        rows[pl.ds(16 + half, 128, stride=2), :] = jnp.where(keep, total, 0.0)
    for y in range(4):
        out_ref[96 * y : 96 * y + 96, :] = rows[64 * y : 64 * y + 96, :].astype(BF16)


def migrate(turned, info):
    return pl.pallas_call(
        migrate_kernel,
        out_shape=jax.ShapeDtypeStruct((384, LANES), BF16),
        scratch_shapes=[pltpu.VMEM((512, LANES), F32), pltpu.VMEM((288, LANES), F32)],
        cost_estimate=pl.CostEstimate(flops=1 << 20, bytes_accessed=1 << 18, transcendentals=0),
        name="migrate",
    )(turned, info)


def bands_kernel(filter_ref, out_ref, table):
    group = lane_ids(32) // 32
    zero = jnp.zeros((32, LANES), F32)

    def tap(t):
        return filter_ref[t].astype(F32) if 0 <= t < 64 else zero

    for m in range(72):
        block = tap(m)
        for jo in range(1, 4):
            block = jnp.where(group == jo, tap(m - jo), block)
        table[pl.ds(128 * (m // 4) + m % 4, 32, stride=4), :] = block
    out_ref[...] = table[...].astype(BF16)


def bands(filter_table):
    return pl.pallas_call(
        bands_kernel,
        out_shape=jax.ShapeDtypeStruct((2304, LANES), BF16),
        scratch_shapes=[pltpu.VMEM((2304, LANES), F32)],
        cost_estimate=pl.CostEstimate(flops=1 << 20, bytes_accessed=1 << 20, transcendentals=0),
        name="bands",
    )(filter_table)


def azimuth_kernel(turned_ref, bands_ref, out_ref, field, pair, result, planes, final):
    arrays = [turned_ref[96 * y : 96 * y + 96, :].astype(F32) for y in range(4)]
    for il, piece in enumerate(swap_blocks(arrays, 32)):
        field[pl.ds(il, 96, stride=4), :] = piece
    field[384:392, :] = jnp.zeros((8, LANES), F32)
    pair[:, :LANES] = field[0:384, :].astype(BF16)
    pair[:, LANES:] = field[8:392, :].astype(BF16)
    total = jnp.zeros((256, LANES), F32)
    for e in range(9):
        total = total + jnp.dot(
            pair[16 * e : 16 * e + 256, :],
            bands_ref[256 * e : 256 * e + 256, :],
            preferred_element_type=F32,
        )
    result[...] = total
    for half in range(2):
        arrays = [result[pl.ds(4 * half + i, 32, stride=8), :] for i in range(4)]
        for jo, piece in enumerate(swap_blocks(arrays, 32)):
            planes[pl.ds(128 * half + jo, 32, stride=4), :] = piece
        turned = planes[128 * half : 128 * half + 128, :].T
        for i in range(4):
            final[pl.ds(4 * half + i, 32, stride=8), :] = turned[32 * i : 32 * i + 32, :]
    out_ref[...] = final[...].astype(BF16)


def azimuth(turned, band_matrix):
    return pl.pallas_call(
        azimuth_kernel,
        out_shape=jax.ShapeDtypeStruct((256, LANES), BF16),
        scratch_shapes=[
            pltpu.VMEM((392, LANES), F32),
            pltpu.VMEM((384, 256), BF16),
            pltpu.VMEM((256, LANES), F32),
            pltpu.VMEM((256, LANES), F32),
            pltpu.VMEM((256, LANES), F32),
        ],
        cost_estimate=pl.CostEstimate(
            flops=2 * 256 * 128 * 2304, bytes_accessed=1 << 20, transcendentals=0
        ),
        name="azimuth",
    )(turned, band_matrix)


def filter_table(recon_filters):
    by_tap = recon_filters.reshape(16, 4, 4, 2, 64).transpose(4, 1, 2, 3, 0)
    real, imag = by_tap[:, :, :, 0], by_tap[:, :, :, 1]
    from_real = jnp.stack([real, imag], -1).reshape(64, 4, 1, 4, 32)
    from_imag = jnp.stack([-imag, real], -1).reshape(64, 4, 1, 4, 32)
    table = jnp.concatenate([from_real, from_imag], 2).reshape(64, 32, 32)
    return jnp.tile(table, (1, 1, 4))


def bin_info(span_offset, span_width, aperture_edges):
    info = jnp.stack([span_offset, span_width, aperture_edges[0], aperture_edges[1]], 0)
    return jnp.repeat(info.reshape(8, 4), 32, axis=1)


def body(echoes, replica, recon_filters, span_offset, span_width, aperture_edges):
    echo_rows = echoes.transpose(2, 0, 1, 3).reshape(2, 16, 8192)
    chunks = compress(echo_rows, replica)
    turned = lax.all_to_all(chunks.reshape(128, 4, LANES), "pulse", 0, 0, tiled=True)
    info = bin_info(span_offset, span_width, aperture_edges)
    band_matrix = bands(filter_table(recon_filters))
    corrected = migrate(turned.reshape(512, LANES), info)
    gathered = lax.all_to_all(corrected.reshape(4, 96, LANES), "chan", 0, 0, tiled=True)
    image = azimuth(gathered.reshape(384, LANES), band_matrix)
    return image.reshape(16, 2, 8, LANES)


def solution(mesh):
    return jax.shard_map(
        body,
        mesh=mesh,
        in_specs=(
            P("chan", "pulse", None, None),
            P(),
            P(),
            P("pulse"),
            P("pulse"),
            P(None, "pulse"),
        ),
        out_specs=P(None, None, "pulse", "chan"),
        check_vma=False,
    )
```

time: 188 us -> 56.8 us (0.30); the launches traced: 184 us -> 55.8 us
  local copies, waits for them, and re-layouts: 130 us -> 6.23 us
  starting transfers between devices: 33.3 us -> 24.7 us
  Pallas kernels: 0 us -> 8.41 us
  other arithmetic: 6.3 us -> 0.13 us
  waiting for transfers between devices: 10.1 us -> 16.2 us
  matrix products: 4.09 us -> 0 us
    another operation x10 -> x5, local copies, waits for them, and re-layouts: 55.3 us -> 2.01 us  [the longest x2 1.79 us: filter_table(): return jnp.tile(table, (1, 1, 4))]
    unnamed x46 -> x15, local copies, waits for them, and re-layouts: 22.6 us -> 2.02 us
    transpose x3 -> x0, local copies, waits for them, and re-layouts: 18.1 us -> none  [the longest x1 14.9 us: azimuth(): window.transpose(2, 3, 0, 1, 4, 5)]
    all_to_all x5 -> x0, local copies, waits for them, and re-layouts: 15.6 us -> none  [the longest x3 14.3 us: body(): lax.all_to_all(compressed, 'pulse', split_axis=2, concat_axis=3, tiled=True)]
    ppermute x3 -> x0, starting transfers between devices: 8.77 us -> none  [the longest x1 3.65 us: padded_2(): lax.ppermute(tail, axis, [(i, (i + 1) % count) for i in range(ends)])]
    pallas_call x0 -> x4, Pallas kernels: none -> 8.41 us  [the longest x1 2.61 us: azimuth(): pl.pallas_call(azimuth_kernel, out_shape=jax.ShapeDtypeStruct((256, LANES...]
    all_to_all x2, waiting for transfers between devices: 8.02 us -> 16.2 us  [the longest x1 15.5 us: body(): lax.all_to_all(chunks.reshape(128, 4, LANES), 'pulse', 0, 0, tiled=True)]
    reshape x7 -> x3, local copies, waits for them, and re-layouts: 8.1 us -> 2.1 us  [the longest x1 1.35 us: body(): echo_rows = echoes.transpose(2, 0, 1, 3).reshape(2, 16, 8192)]
  transfers between devices with their start and end apart: 5 -> 2, of which waited for: 2 -> 2; matrix products, arithmetic and copies ran while one was open for 9% -> 5% of each run, Pallas kernels for 0% -> 4%
where the time goes in v1:
time: 56.8 us; the launch traced here: 55.8 us
  starting transfers between devices  24.7 us (43%)
  waiting for transfers between devices  16.2 us (29%)
  Pallas kernels  8.41 us (15%)
  local copies, waits for them, and re-layouts  6.23 us (11%)
    all_to_all x1, starting transfers between devices, body(): lax.all_to_all(chunks.reshape(128, 4, LANES), 'pulse', 0, 0, tiled=True)  20.5 us
    all_to_all x1, waiting for transfers between devices, body(): lax.all_to_all(chunks.reshape(128, 4, LANES), 'pulse', 0, 0, tiled=True)  15.5 us
    all_to_all x1, starting transfers between devices, body(): lax.all_to_all(corrected.reshape(4, 96, LANES), 'chan', 0, 0, tiled=True)  4.18 us
    pallas_call x1, Pallas kernels, azimuth(): pl.pallas_call(azimuth_kernel, out_shape=jax.ShapeDtypeStruct((256, LANES...  2.61 us
    pallas_call x1, Pallas kernels, bands(): pl.pallas_call(bands_kernel, out_shape=jax.ShapeDtypeStruct((2304, LANES)...  2.07 us
    unnamed x15, local copies, waits for them, and re-layouts  2.02 us
    pallas_call x1, Pallas kernels, migrate(): pl.pallas_call(migrate_kernel, out_shape=jax.ShapeDtypeStruct((384, LANES...  1.88 us
    pallas_call x1, Pallas kernels, compress(): pl.pallas_call(compress_kernel, out_shape=jax.ShapeDtypeStruct((512, LANE...  1.85 us
  transfers between devices with their start and end apart: 2, of which 2 were waited for; matrix products, arithmetic and copies ran while one was open for 5% of the time, Pallas kernels for 4%

profile of v1, /device:TPU:1, one launch (start us, length us, event | category | flops | bytes accessed | tf_op | source)
XLA Modules:
  0.0 55.8 jit_solution(10805041745850375193)
XLA Ops:
  0.0 0.0 copy-start
  0.0 1.3 %copy.20.echo_ref = bf16[2,16,8192]{2,1,0:T(8,128)(2,1)S(1)} copy(bf16[2,16,8192]{2,0,1:T(2,128)(2,1)} %bitcast.28) | data formatting | bytes 1048576 | tf_op jit(solution)/shard_map/reshape | solution.py:223
  1.4 0.0 copy-done
  1.4 1.9 %compress.1 = bf16[512,128]{1,0:T(8,128)(2,1)} custom-call(bf16[2,16,8192]{2,1,0:T(8,128)(2,1)S(1)} %copy.20.echo_ref, bf16[2,4096]{1,0:T(2,128)(2,1)S(1)} %copy-done), custom_call_target="tpu_custom_call" | custom-call | flops 603979776 | bytes 1048576 | tf_op jit(solution)/shard_map/compress/pallas_call | solution.py:84
  3.2 0.0 copy-start.3
  3.2 20.5 %all-to-all-start = ((bf16[128,4,128]{2,1,0:T(4,128)(2,1)}), bf16[128,4,128]{2,1,0:T(4,128)(2,1)S(1)}, u32[]{:S(2)}, u32[]{:S(2)}) async-start(bf16[128,4,128]{2,1,0:T(4,128)(2,1)} %bitcast.2), calls=%async_computation | async-start | bytes 262144 | tf_op jit(solution)/shard_map/all_to_all | solution.py:225
  23.7 0.0 copy-done.3
  23.8 0.1 copy.15
  23.9 0.1 pad_maximum_fusion.1
  23.9 0.1 copy.16
  24.0 0.0 copy-start.6
  24.0 0.1 copy.17
  24.2 0.0 copy-start.4
  24.2 0.0 copy-start.5
  24.2 0.5 copy-done.6
  24.7 0.1 copy-done.4
  24.8 0.0 copy-done.5
  24.9 0.1 reshape.50
  24.9 0.1 broadcast_in_dim.3
  25.0 0.7 %reshape.51.info_ref = s32[8,128]{1,0:T(8,128)} reshape(s32[8,4,32]{2,1,0:T(4,128)S(1)} %broadcast_in_dim.3) | data formatting | bytes 8192 | tf_op jit(solution)/shard_map/reshape | solution.py:219
  25.7 15.5 %all-to-all-done = bf16[128,4,128]{2,1,0:T(4,128)(2,1)S(1)} async-done(((bf16[128,4,128]{2,1,0:T(4,128)(2,1)}), bf16[128,4,128]{2,1,0:T(4,128)(2,1)S(1)}, u32[]{:S(2)}, u32[]{:S(2)}) %all-to-all-start) | async-done | bytes 131104 | tf_op jit(solution)/shard_map/all_to_all | solution.py:225
  41.1 0.0 copy-start.1
  41.1 0.6 %copy-done.1 = bf16[128,4,128]{2,1,0:T(4,128)(2,1)} copy-done((bf16[128,4,128]{2,1,0:T(4,128)(2,1)}, bf16[128,4,128]{2,1,0:T(4,128)(2,1)S(1)}, u32[]{:S(2)}) %copy-start.1) | copy-done | bytes 131096
  41.8 1.9 %migrate.1 = bf16[384,128]{1,0:T(8,128)(2,1)} custom-call(bf16[512,128]{1,0:T(8,128)(2,1)} %bitcast.27, s32[8,128]{1,0:T(8,128)} %reshape.51.info_ref), custom_call_target="tpu_custom_call" | custom-call | flops 1048576 | bytes 262144 | tf_op jit(solution)/shard_map/migrate/pallas_call | solution.py:131
  43.7 4.2 %all-to-all-start.1 = ((bf16[4,96,128]{2,1,0:T(8,128)(2,1)}), bf16[4,96,128]{2,1,0:T(8,128)(2,1)S(1)}, u32[]{:S(2)}, u32[]{:S(2)}) async-start(bf16[4,96,128]{2,1,0:T(8,128)(2,1)} %bitcast.31), calls=%async_computation.1 | async-start | bytes 196608 | tf_op jit(solution)/shard_map/all_to_all | solution.py:229
  47.9 0.1 pad_maximum_fusion
  47.9 0.2 tile.11
  48.1 1.6 %copy.19.filter_ref = bf16[64,32,128]{2,1,0:T(8,128)(2,1)} copy(bf16[64,32,128]{0,2,1:T(8,128)(2,1)S(1)} %bitcast.23) | data formatting | bytes 1048576 | tf_op jit(solution)/shard_map/tile | solution.py:214
  49.8 2.1 %bands.1.bands_ref = bf16[2304,128]{1,0:T(8,128)(2,1)} custom-call(bf16[64,32,128]{2,1,0:T(8,128)(2,1)} %copy.19.filter_ref), custom_call_target="tpu_custom_call" | custom-call | flops 1048576 | bytes 1048576 | tf_op jit(solution)/shard_map/bands/pallas_call | solution.py:156
  51.8 0.7 %all-to-all-done.1 = bf16[4,96,128]{2,1,0:T(8,128)(2,1)S(1)} async-done(((bf16[4,96,128]{2,1,0:T(8,128)(2,1)}), bf16[4,96,128]{2,1,0:T(8,128)(2,1)S(1)}, u32[]{:S(2)}, u32[]{:S(2)}) %all-to-all-start.1) | async-done | bytes 98336 | tf_op jit(solution)/shard_map/all_to_all | solution.py:229
  52.5 0.0 copy-start.2
  52.5 0.6 %copy-done.2 = bf16[4,96,128]{2,1,0:T(8,128)(2,1)} copy-done((bf16[4,96,128]{2,1,0:T(8,128)(2,1)}, bf16[4,96,128]{2,1,0:T(8,128)(2,1)S(1)}, u32[]{:S(2)}) %copy-start.2) | copy-done | bytes 98328
  53.2 2.6 %azimuth.1 = bf16[256,128]{1,0:T(8,128)(2,1)} custom-call(bf16[384,128]{1,0:T(8,128)(2,1)} %bitcast.32, bf16[2304,128]{1,0:T(8,128)(2,1)} %bands.1.bands_ref), custom_call_target="tpu_custom_call" | custom-call | flops 150994944 | bytes 1048576 | tf_op jit(solution)/shard_map/azimuth/pallas_call | solution.py:191
  (4 shorter events, 0.1 us)
Async XLA Ops:
  0.0 1.4 %copy-start = (bf16[2,4096]{1,0:T(2,128)(2,1)S(1)}, bf16[2,4096]{1,0:T(2,128)(2,1)}, u32[]{:S(2)}) copy-start(bf16[2,4096]{1,0:T(2,128)(2,1)} %replica_ref.1) | copy-start | bytes 49156
  3.2 20.5 %copy-start.3 = (bf16[16,16,2,64]{3,2,1,0:T(2,128)(2,1)S(1)}, bf16[16,16,2,64]{3,2,1,0:T(2,128)(2,1)}, u32[]{:S(2)}) copy-start(bf16[16,16,2,64]{3,2,1,0:T(2,128)(2,1)} %param.8) | copy-start | bytes 196612
  3.2 37.9 %all-to-all-start = ((bf16[128,4,128]{2,1,0:T(4,128)(2,1)}), bf16[128,4,128]{2,1,0:T(4,128)(2,1)S(1)}, u32[]{:S(2)}, u32[]{:S(2)}) async-start(bf16[128,4,128]{2,1,0:T(4,128)(2,1)} %bitcast.2), calls=%async_computation | async-start | bytes 262144 | tf_op jit(solution)/shard_map/all_to_all | solution.py:225
  24.0 0.7 %copy-start.6 = (s32[8]{0:T(128)S(1)}, s32[8]{0:T(128)}, u32[]{:S(2)}) copy-start(s32[8]{0:T(128)} %param.9) | copy-start | bytes 100
  24.2 0.7 %copy-start.4 = (s32[2,8]{1,0:T(2,128)S(1)}, s32[2,8]{1,0:T(2,128)}, u32[]{:S(2)}) copy-start(s32[2,8]{1,0:T(2,128)} %param.11) | copy-start | bytes 196
  24.2 0.7 %copy-start.5 = (s32[8]{0:T(128)S(1)}, s32[8]{0:T(128)}, u32[]{:S(2)}) copy-start(s32[8]{0:T(128)} %param.10) | copy-start | bytes 100
  41.1 0.7 %copy-start.1 = (bf16[128,4,128]{2,1,0:T(4,128)(2,1)}, bf16[128,4,128]{2,1,0:T(4,128)(2,1)S(1)}, u32[]{:S(2)}) copy-start(bf16[128,4,128]{2,1,0:T(4,128)(2,1)S(1)} %all-to-all-done) | copy-start | bytes 393220
  43.7 8.8 %all-to-all-start.1 = ((bf16[4,96,128]{2,1,0:T(8,128)(2,1)}), bf16[4,96,128]{2,1,0:T(8,128)(2,1)S(1)}, u32[]{:S(2)}, u32[]{:S(2)}) async-start(bf16[4,96,128]{2,1,0:T(8,128)(2,1)} %bitcast.31), calls=%async_computation.1 | async-start | bytes 196608 | tf_op jit(solution)/shard_map/all_to_all | solution.py:229
  52.5 0.6 %copy-start.2 = (bf16[4,96,128]{2,1,0:T(8,128)(2,1)}, bf16[4,96,128]{2,1,0:T(8,128)(2,1)S(1)}, u32[]{:S(2)}) copy-start(bf16[4,96,128]{2,1,0:T(8,128)(2,1)S(1)} %all-to-all-done.1) | copy-start | bytes 294916

commit v2 on v1

--- a/solution.py
+++ b/solution.py
@@ -1,10 +1,9 @@
-import functools
-
 import jax
 import jax.numpy as jnp
 from jax import lax
 from jax.experimental import pallas as pl
 from jax.experimental.pallas import tpu as pltpu
+from jax.sharding import Mesh
 from jax.sharding import PartitionSpec as P
 
 F32 = jnp.float32
@@ -75,23 +74,23 @@
     for w, piece in enumerate(swap_blocks(pieces, 16)):
         rows[32 * w : 32 * w + 32, :] = piece
     rows[256:264, :] = jnp.zeros((8, LANES), F32)
-    for k in range(4):
-        chunks[pl.ds(k, 128, stride=4), :] = rows[pl.ds(k, 128, stride=2), :]
-    out_ref[...] = chunks[...].astype(BF16)
+    for k in range(6):
+        chunks[:, k, :] = rows[pl.ds(k, 64, stride=4), :]
+    out_ref[...] = chunks[:, 0:6, :].astype(BF16)
 
 
 def compress(echo_rows, replica):
     return pl.pallas_call(
         compress_kernel,
-        out_shape=jax.ShapeDtypeStruct((512, LANES), BF16),
+        out_shape=jax.ShapeDtypeStruct((64, 6, LANES), BF16),
         scratch_shapes=[
             pltpu.VMEM((256, 4608), BF16),
             pltpu.VMEM((256, 4608), BF16),
             pltpu.VMEM((256, LANES), F32),
             pltpu.VMEM((264, LANES), F32),
-            pltpu.VMEM((512, LANES), F32),
+            pltpu.VMEM((64, 8, LANES), F32),
         ],
-        compiler_params=pltpu.CompilerParams(vmem_limit_bytes=24 << 20),
+        compiler_params=pltpu.CompilerParams(vmem_limit_bytes=16 << 20),
         cost_estimate=pl.CostEstimate(
             flops=2 * 256 * 256 * 4608, bytes_accessed=1 << 20, transcendentals=0
         ),
@@ -99,42 +98,28 @@
     )(echo_rows, replica)
 
 
-def migrate_kernel(turned_ref, info_ref, out_ref, quads, rows):
-    quads[...] = turned_ref[...].astype(F32)
-    quad = [quads[pl.ds(k, 128, stride=4), :] for k in range(4)]
-    lane = lane_ids(128)
-    group = lane // 32
-    pulse = 4 * lax.broadcasted_iota(jnp.int32, (128, LANES), 0) + lane % 4
-    shifted = [quad]
-    for f in range(1, 4):
-        rolled = [pltpu.roll(q, LANES - 32 * f, 1) for q in quad]
-        shifted.append([jnp.where(group < 4 - f, rolled[k], rolled[k + 1]) for k in range(3)])
-    rows[0:16, :] = jnp.zeros((16, LANES), F32)
-    rows[272:288, :] = jnp.zeros((16, LANES), F32)
-    for half in range(2):
-        first = info_ref[half : half + 1, :]
-        width = info_ref[2 + half : 3 + half, :]
-        low = info_ref[4 + half : 5 + half, :]
-        high = info_ref[6 + half : 7 + half, :]
-        total = jnp.zeros((128, LANES), F32)
-        for step in range(8):
-            inside = (first <= step) & (step < first + width)
-            total = total + jnp.where(inside, shifted[step % 4][half + step // 4], 0.0)
-        total = total * (1.0 / width.astype(F32))
-        keep = (pulse >= low) & (pulse < 512 - high)
-        rows[pl.ds(16 + half, 128, stride=2), :] = jnp.where(keep, total, 0.0)
+def regroup_kernel(turned_ref, out_ref, quads, rows):
+    quads[:, 0:6, :] = turned_ref[...].astype(F32)
+    for core in range(2):
+        rows[core, 0:16, :] = jnp.zeros((16, LANES), F32)
+        rows[core, 272:288, :] = jnp.zeros((16, LANES), F32)
+        for k in range(4):
+            rows[core, pl.ds(16 + k, 64, stride=4), :] = quads[:, 2 * core + k, :]
     for y in range(4):
-        out_ref[96 * y : 96 * y + 96, :] = rows[64 * y : 64 * y + 96, :].astype(BF16)
-
-
-def migrate(turned, info):
-    return pl.pallas_call(
-        migrate_kernel,
-        out_shape=jax.ShapeDtypeStruct((384, LANES), BF16),
-        scratch_shapes=[pltpu.VMEM((512, LANES), F32), pltpu.VMEM((288, LANES), F32)],
-        cost_estimate=pl.CostEstimate(flops=1 << 20, bytes_accessed=1 << 18, transcendentals=0),
-        name="migrate",
-    )(turned, info)
+        for core in range(2):
+            at = 96 * (2 * y + core)
+            out_ref[at : at + 96, :] = rows[core, 64 * y : 64 * y + 96, :].astype(BF16)
+
+
+def regroup(turned):
+    return pl.pallas_call(
+        regroup_kernel,
+        out_shape=jax.ShapeDtypeStruct((768, LANES), BF16),
+        scratch_shapes=[pltpu.VMEM((64, 8, LANES), F32), pltpu.VMEM((2, 288, LANES), F32)],
+        compiler_params=pltpu.CompilerParams(vmem_limit_bytes=8 << 20),
+        cost_estimate=pl.CostEstimate(flops=1 << 18, bytes_accessed=1 << 18, transcendentals=0),
+        name="regroup",
+    )(turned)
 
 
 def bands_kernel(filter_ref, out_ref, table):
@@ -157,15 +142,49 @@
         bands_kernel,
         out_shape=jax.ShapeDtypeStruct((2304, LANES), BF16),
         scratch_shapes=[pltpu.VMEM((2304, LANES), F32)],
+        compiler_params=pltpu.CompilerParams(vmem_limit_bytes=8 << 20),
         cost_estimate=pl.CostEstimate(flops=1 << 20, bytes_accessed=1 << 20, transcendentals=0),
         name="bands",
     )(filter_table)
 
 
-def azimuth_kernel(turned_ref, bands_ref, out_ref, field, pair, result, planes, final):
-    arrays = [turned_ref[96 * y : 96 * y + 96, :].astype(F32) for y in range(4)]
-    for il, piece in enumerate(swap_blocks(arrays, 32)):
-        field[pl.ds(il, 96, stride=4), :] = piece
+def migrate(quad, info_ref, pulse):
+    rows = quad[0].shape[0]
+    group = lane_ids(rows) // 32
+    shifted = [quad]
+    for f in range(1, 4):
+        rolled = [pltpu.roll(q, LANES - 32 * f, 1) for q in quad]
+        shifted.append([jnp.where(group < 4 - f, rolled[k], rolled[k + 1]) for k in range(3)])
+    halves = []
+    for half in range(2):
+        first = info_ref[half : half + 1, :]
+        width = info_ref[2 + half : 3 + half, :]
+        low = info_ref[4 + half : 5 + half, :]
+        high = info_ref[6 + half : 7 + half, :]
+        total = jnp.zeros((rows, LANES), F32)
+        for step in range(8):
+            inside = (first <= step) & (step < first + width)
+            total = total + jnp.where(inside, shifted[step % 4][half + step // 4], 0.0)
+        total = total * (1.0 / width.astype(F32))
+        halves.append(jnp.where((pulse >= low) & (pulse < high), total, 0.0))
+    return halves
+
+
+def azimuth_kernel(
+    turned_ref, info_ref, bands_ref, out_ref, quads, field, pair, result, planes, final
+):
+    quads[...] = turned_ref[...].astype(F32)
+    slot = lax.broadcasted_iota(jnp.int32, (24, LANES), 0)
+    for core in range(2):
+        pulse = 8 * slot + 4 * core + lane_ids(24) % 4
+        halves = []
+        for y in range(4):
+            at = 96 * (2 * y + core)
+            quad = [quads[pl.ds(at + k, 24, stride=4), :] for k in range(4)]
+            halves.append(migrate(quad, info_ref, pulse))
+        for half in range(2):
+            for il, piece in enumerate(swap_blocks([h[half] for h in halves], 32)):
+                field[pl.ds(8 * core + 4 * half + il, 24, stride=16), :] = piece
     field[384:392, :] = jnp.zeros((8, LANES), F32)
     pair[:, :LANES] = field[0:384, :].astype(BF16)
     pair[:, LANES:] = field[8:392, :].astype(BF16)
@@ -187,11 +206,12 @@
     out_ref[...] = final[...].astype(BF16)
 
 
-def azimuth(turned, band_matrix):
+def azimuth(turned, info, band_matrix):
     return pl.pallas_call(
         azimuth_kernel,
         out_shape=jax.ShapeDtypeStruct((256, LANES), BF16),
         scratch_shapes=[
+            pltpu.VMEM((768, LANES), F32),
             pltpu.VMEM((392, LANES), F32),
             pltpu.VMEM((384, 256), BF16),
             pltpu.VMEM((256, LANES), F32),
@@ -201,8 +221,9 @@
         cost_estimate=pl.CostEstimate(
             flops=2 * 256 * 128 * 2304, bytes_accessed=1 << 20, transcendentals=0
         ),
+        compiler_params=pltpu.CompilerParams(vmem_limit_bytes=8 << 20),
         name="azimuth",
-    )(turned, band_matrix)
+    )(turned, info, band_matrix)
 
 
 def filter_table(recon_filters):
@@ -215,34 +236,41 @@
 
 
 def bin_info(span_offset, span_width, aperture_edges):
-    info = jnp.stack([span_offset, span_width, aperture_edges[0], aperture_edges[1]], 0)
+    origin = 128 * lax.axis_index("chan") - 32
+    info = jnp.stack(
+        [span_offset, span_width, aperture_edges[0] - origin, 512 - aperture_edges[1] - origin], 0
+    )
     return jnp.repeat(info.reshape(8, 4), 32, axis=1)
 
 
 def body(echoes, replica, recon_filters, span_offset, span_width, aperture_edges):
     echo_rows = echoes.transpose(2, 0, 1, 3).reshape(2, 16, 8192)
     chunks = compress(echo_rows, replica)
-    turned = lax.all_to_all(chunks.reshape(128, 4, LANES), "pulse", 0, 0, tiled=True)
+    turned = lax.all_to_all(chunks, "slot", 0, 0, tiled=True)
     info = bin_info(span_offset, span_width, aperture_edges)
     band_matrix = bands(filter_table(recon_filters))
-    corrected = migrate(turned.reshape(512, LANES), info)
-    gathered = lax.all_to_all(corrected.reshape(4, 96, LANES), "chan", 0, 0, tiled=True)
-    image = azimuth(gathered.reshape(384, LANES), band_matrix)
+    windows = regroup(turned)
+    gathered = lax.all_to_all(
+        windows.reshape(8, 96, LANES), ("chan", "core"), 0, 0, tiled=True
+    )
+    image = azimuth(gathered.reshape(768, LANES), info, band_matrix)
     return image.reshape(16, 2, 8, LANES)
 
 
 def solution(mesh):
+    split = Mesh(mesh.devices.reshape(64, 2, 4), ("slot", "core", "chan"))
+    pulse = ("slot", "core")
     return jax.shard_map(
         body,
-        mesh=mesh,
+        mesh=split,
         in_specs=(
-            P("chan", "pulse", None, None),
+            P("chan", pulse, None, None),
             P(),
             P(),
-            P("pulse"),
-            P("pulse"),
-            P(None, "pulse"),
+            P(pulse),
+            P(pulse),
+            P(None, pulse),
         ),
-        out_specs=P(None, None, "pulse", "chan"),
+        out_specs=P(None, None, pulse, "chan"),
         check_vma=False,
     )

time: 56.8 us -> 53.1 us (0.935); the launches traced: 55.8 us -> 52.8 us
  Pallas kernels: 8.41 us -> 4.73 us
  starting transfers between devices: 24.7 us -> 27 us
  local copies, waits for them, and re-layouts: 6.23 us -> 4.2 us
    all_to_all x2, starting transfers between devices: 24.7 us -> 27 us  [the longest x1 19.2 us: body(): turned = lax.all_to_all(chunks, 'slot', 0, 0, tiled=True)]
    pallas_call x1, Pallas kernels: 2.07 us -> 0.2 us  [bands(): pl.pallas_call(bands_kernel, out_shape=jax.ShapeDtypeStruct((2304, LANES)...]
    pallas_call x2, Pallas kernels: 3.73 us -> 2.77 us  [the longest x1 1.94 us: compress(): pl.pallas_call(compress_kernel, out_shape=jax.ShapeDtypeStruct((64, 6, LA...]
    pallas_call x1, Pallas kernels: 2.61 us -> 1.75 us  [azimuth(): pl.pallas_call(azimuth_kernel, out_shape=jax.ShapeDtypeStruct((256, LANES...]
    another operation x2, local copies, waits for them, and re-layouts: 1.79 us -> 0.99 us  [filter_table(): return jnp.tile(table, (1, 1, 4))]
    unnamed x15 -> x11, local copies, waits for them, and re-layouts: 2.02 us -> 1.39 us
    reshape x2, local copies, waits for them, and re-layouts: 0.76 us -> 0.16 us  [bin_info(): return jnp.repeat(info.reshape(8, 4), 32, axis=1)]
  transfers between devices with their start and end apart: 2 -> 2, of which waited for: 2 -> 2; matrix products, arithmetic and copies ran while one was open for 5% -> 3% of each run, Pallas kernels for 4% -> 0%
where the time goes in v2:
time: 53.1 us; the launch traced here: 52.8 us
  starting transfers between devices  27 us (51%)
  waiting for transfers between devices  16.5 us (31%)
  Pallas kernels  4.73 us (9%)
  local copies, waits for them, and re-layouts  4.2 us (8%)
    all_to_all x1, starting transfers between devices, body(): turned = lax.all_to_all(chunks, 'slot', 0, 0, tiled=True)  19.2 us
    all_to_all x1, waiting for transfers between devices, body(): turned = lax.all_to_all(chunks, 'slot', 0, 0, tiled=True)  12.9 us
    all_to_all x1, starting transfers between devices, body(): lax.all_to_all(windows.reshape(8, 96, LANES), ('chan', 'core'), 0, 0, til...  7.81 us
    all_to_all x1, waiting for transfers between devices, body(): lax.all_to_all(windows.reshape(8, 96, LANES), ('chan', 'core'), 0, 0, til...  3.67 us
    pallas_call x1, Pallas kernels, compress(): pl.pallas_call(compress_kernel, out_shape=jax.ShapeDtypeStruct((64, 6, LA...  1.94 us
    pallas_call x1, Pallas kernels, azimuth(): pl.pallas_call(azimuth_kernel, out_shape=jax.ShapeDtypeStruct((256, LANES...  1.75 us
    unnamed x11, local copies, waits for them, and re-layouts  1.39 us
    reshape x1, local copies, waits for them, and re-layouts, body(): echo_rows = echoes.transpose(2, 0, 1, 3).reshape(2, 16, 8192)  1.35 us
  transfers between devices with their start and end apart: 2, of which 2 were waited for; matrix products, arithmetic and copies ran while one was open for 3% of the time, Pallas kernels for 0%

profile of v2, /device:TPU:1, one launch (start us, length us, event | category | flops | bytes accessed | tf_op | source)
XLA Modules:
  0.0 52.8 jit_solution(9354623744967152188)
XLA Ops:
  0.0 0.0 copy-start
  0.0 1.3 %copy.20.echo_ref = bf16[2,16,8192]{2,1,0:T(8,128)(2,1)S(1)} copy(bf16[2,16,8192]{2,0,1:T(2,128)(2,1)} %bitcast.26) | data formatting | bytes 1048576 | tf_op jit(solution)/shard_map/reshape | solution.py:247
  1.4 0.0 copy-done
  1.4 1.9 %compress.1 = bf16[64,6,128]{2,1,0:T(8,128)(2,1)} custom-call(bf16[2,16,8192]{2,1,0:T(8,128)(2,1)S(1)} %copy.20.echo_ref, bf16[2,4096]{1,0:T(2,128)(2,1)S(1)} %copy-done), custom_call_target="tpu_custom_call" | custom-call | flops 603979776 | bytes 1048576 | tf_op jit(solution)/shard_map/compress/pallas_call | solution.py:83
  3.3 0.0 copy-start.1
  3.3 19.2 %all-to-all-start = ((bf16[64,6,128]{2,1,0:T(8,128)(2,1)}), bf16[64,6,128]{2,1,0:T(8,128)(2,1)S(1)}, u32[]{:S(2)}, u32[]{:S(2)}) async-start(bf16[64,6,128]{2,1,0:T(8,128)(2,1)} %compress.1), calls=%async_computation | async-start | bytes 262144 | tf_op jit(solution)/shard_map/all_to_all | solution.py:249
  22.6 0.0 copy-done.1
  22.6 0.1 copy.15
  22.7 0.1 pad_maximum_fusion.1
  22.7 0.1 copy.16
  22.8 0.1 copy.17
  23.0 0.0 copy-start.2
  23.0 0.7 %copy-done.2 = s32[2,8]{1,0:T(2,128)S(1)} copy-done((s32[2,8]{1,0:T(2,128)S(1)}, s32[2,8]{1,0:T(2,128)}, u32[]{:S(2)}) %copy-start.2) | copy-done | bytes 88
  23.7 12.9 %all-to-all-done.turned_ref = bf16[64,6,128]{2,1,0:T(8,128)(2,1)S(1)} async-done(((bf16[64,6,128]{2,1,0:T(8,128)(2,1)}), bf16[64,6,128]{2,1,0:T(8,128)(2,1)S(1)}, u32[]{:S(2)}, u32[]{:S(2)}) %all-to-all-start) | async-done | bytes 98336 | tf_op jit(solution)/shard_map/all_to_all | solution.py:249
  36.5 0.8 %regroup.1 = bf16[768,128]{1,0:T(8,128)(2,1)} custom-call(bf16[64,6,128]{2,1,0:T(8,128)(2,1)S(1)} %all-to-all-done.turned_ref), custom_call_target="tpu_custom_call" | custom-call | flops 262144 | bytes 262144 | tf_op jit(solution)/shard_map/regroup/pallas_call | solution.py:115
  37.4 7.8 %all-to-all-start.1 = ((bf16[8,96,128]{2,1,0:T(8,128)(2,1)}), bf16[8,96,128]{2,1,0:T(8,128)(2,1)S(1)}, u32[]{:S(2)}, u32[]{:S(2)}) async-start(bf16[8,96,128]{2,1,0:T(8,128)(2,1)} %bitcast.2), calls=%async_computation.1 | async-start | bytes 393216 | tf_op jit(solution)/shard_map/all_to_all | solution.py:253
  45.2 0.1 pad_maximum_fusion
  45.2 0.2 tile.11
  45.4 0.8 %copy.19.filter_ref = bf16[64,32,128]{2,1,0:T(8,128)(2,1)S(1)} copy(bf16[64,32,128]{0,2,1:T(8,128)(2,1)S(1)} %bitcast.22) | data formatting | bytes 1048576 | tf_op jit(solution)/shard_map/tile | solution.py:235
  46.3 0.0 copy-start.3
  46.3 0.0 copy-start.4
  46.3 0.6 %copy-done.3 = s32[8]{0:T(128)S(1)} copy-done((s32[8]{0:T(128)S(1)}, s32[8]{0:T(128)}, u32[]{:S(2)}) %copy-start.3) | copy-done | bytes 56
  46.9 0.0 copy-done.4
  46.9 0.1 reshape.44
  47.0 0.1 broadcast_in_dim.3
  47.1 0.1 reshape.45.info_ref
  47.2 0.2 bands.1.bands_ref
  47.4 3.7 %all-to-all-done.1 = bf16[8,96,128]{2,1,0:T(8,128)(2,1)S(1)} async-done(((bf16[8,96,128]{2,1,0:T(8,128)(2,1)}), bf16[8,96,128]{2,1,0:T(8,128)(2,1)S(1)}, u32[]{:S(2)}, u32[]{:S(2)}) %all-to-all-start.1) | async-done | bytes 196640 | tf_op jit(solution)/shard_map/all_to_all | solution.py:253
  51.1 1.8 %azimuth.1 = bf16[256,128]{1,0:T(8,128)(2,1)} custom-call(bf16[768,128]{1,0:T(8,128)(2,1)S(1)} %bitcast.21, s32[8,128]{1,0:T(8,128)S(1)} %reshape.45.info_ref, bf16[2304,128]{1,0:T(8,128)(2,1)S(1)} %bands.1.bands_ref), custom_call_target="tpu_custom_call" | custom-call | flops 150994944 | bytes 1048576 | tf_op jit(solution)/shard_map/azimuth/pallas_call | solution.py:210
  (5 shorter events, 0.1 us)
Async XLA Ops:
  0.0 1.4 %copy-start = (bf16[2,4096]{1,0:T(2,128)(2,1)S(1)}, bf16[2,4096]{1,0:T(2,128)(2,1)}, u32[]{:S(2)}) copy-start(bf16[2,4096]{1,0:T(2,128)(2,1)} %replica_ref.1) | copy-start | bytes 49156
  3.3 19.3 %copy-start.1 = (bf16[16,16,2,64]{3,2,1,0:T(2,128)(2,1)S(1)}, bf16[16,16,2,64]{3,2,1,0:T(2,128)(2,1)}, u32[]{:S(2)}) copy-start(bf16[16,16,2,64]{3,2,1,0:T(2,128)(2,1)} %param.8) | copy-start | bytes 196612
  3.3 33.2 %all-to-all-start = ((bf16[64,6,128]{2,1,0:T(8,128)(2,1)}), bf16[64,6,128]{2,1,0:T(8,128)(2,1)S(1)}, u32[]{:S(2)}, u32[]{:S(2)}) async-start(bf16[64,6,128]{2,1,0:T(8,128)(2,1)} %compress.1), calls=%async_computation | async-start | bytes 262144 | tf_op jit(solution)/shard_map/all_to_all | solution.py:249
  23.0 0.7 %copy-start.2 = (s32[2,8]{1,0:T(2,128)S(1)}, s32[2,8]{1,0:T(2,128)}, u32[]{:S(2)}) copy-start(s32[2,8]{1,0:T(2,128)} %param.11) | copy-start | bytes 196
  37.4 13.7 %all-to-all-start.1 = ((bf16[8,96,128]{2,1,0:T(8,128)(2,1)}), bf16[8,96,128]{2,1,0:T(8,128)(2,1)S(1)}, u32[]{:S(2)}, u32[]{:S(2)}) async-start(bf16[8,96,128]{2,1,0:T(8,128)(2,1)} %bitcast.2), calls=%async_computation.1 | async-start | bytes 393216 | tf_op jit(solution)/shard_map/all_to_all | solution.py:253
  46.3 0.7 %copy-start.3 = (s32[8]{0:T(128)S(1)}, s32[8]{0:T(128)}, u32[]{:S(2)}) copy-start(s32[8]{0:T(128)} %param.10) | copy-start | bytes 100
  46.3 0.7 %copy-start.4 = (s32[8]{0:T(128)S(1)}, s32[8]{0:T(128)}, u32[]{:S(2)}) copy-start(s32[8]{0:T(128)} %param.9) | copy-start | bytes 100

commit v3 on v2

--- a/solution.py
+++ b/solution.py
@@ -10,6 +10,9 @@
 BF16 = jnp.bfloat16
 LANES = 128
 NT = (((1,), (1,)), ((), ()))
+FIRST = 41
+LAST = ((2, 0), (2, 1), (3, 0), (3, 1), (0, 0), (0, 1), (1, 0), (1, 1))
+SEGMENTS = ((0, FIRST, 64 - FIRST), (64 - FIRST, 0, FIRST))
 
 
 def lane_ids(rows):
@@ -34,7 +37,20 @@
     return arrays
 
 
-def compress_kernel(echo_ref, replica_ref, out_ref, taps, windows, parts, rows, chunks):
+def compress_kernel(
+    echo_ref, replica_hbm, out_ref, replica_ref, echo_rows, sems, taps, windows, parts, rows, chunks
+):
+    taps_copy = pltpu.make_async_copy(replica_hbm, replica_ref, sems.at[16])
+    taps_copy.start()
+    copies = [
+        pltpu.make_async_copy(
+            echo_ref.at[row // 4, row % 4], echo_rows.at[pl.ds(2 * row, 2), :], sems.at[row]
+        )
+        for row in range(16)
+    ]
+    for copy in copies:
+        copy.start()
+    taps_copy.wait()
     lane = lane_ids(32)
     shift = 4 * lax.broadcasted_iota(jnp.int32, (32, LANES), 0)
     zero = jnp.zeros((32, LANES), F32)
@@ -63,39 +79,53 @@
                 taps[base : base + 32, (33 + a) * LANES :] = jnp.zeros(
                     (32, (3 - a) * LANES), BF16
                 )
-    for part in range(2):
-        for w in range(8):
-            at = part * 128 + w * 16
-            windows[at : at + 16, :] = echo_ref[part, :, 512 * w : 512 * w + 4608]
+    for copy in copies:
+        copy.wait()
+    for w in range(8):
+        windows[32 * w : 32 * w + 32, :] = echo_rows[:, 512 * w : 512 * w + 4608]
     product = lax.dot_general(taps[...], windows[...], NT, preferred_element_type=F32)
-    parts[0:128, :] = product[:128, :128] - product[128:, 128:]
-    parts[128:256, :] = product[:128, 128:] + product[128:, :128]
-    pieces = [parts[pl.ds(128 * (g % 2) + g // 2, 32, stride=4), :] for g in range(8)]
-    for w, piece in enumerate(swap_blocks(pieces, 16)):
-        rows[32 * w : 32 * w + 32, :] = piece
+    real_lane = lane_ids(128) % 2 == 0
+    for half in range(2):
+        by_real = product[:128, 128 * half : 128 * half + 128]
+        by_imag = product[128:, 128 * half : 128 * half + 128]
+        parts[128 * half : 128 * half + 128, :] = by_real + jnp.where(
+            real_lane, -pltpu.roll(by_imag, LANES - 1, 1), pltpu.roll(by_imag, 1, 1)
+        )
+        pieces = [parts[pl.ds(128 * half + il, 32, stride=4), :] for il in range(4)]
+        for w, piece in enumerate(swap_blocks(pieces, 32)):
+            at = 128 * half + 32 * w
+            rows[at : at + 32, :] = piece
     rows[256:264, :] = jnp.zeros((8, LANES), F32)
-    for k in range(6):
-        chunks[:, k, :] = rows[pl.ds(k, 64, stride=4), :]
+    for at, slot, count in SEGMENTS:
+        for k in range(6):
+            chunks[at : at + count, k, :] = rows[pl.ds(4 * slot + k, count, stride=4), :]
     out_ref[...] = chunks[:, 0:6, :].astype(BF16)
 
 
-def compress(echo_rows, replica):
+def compress(echoes, replica):
     return pl.pallas_call(
         compress_kernel,
         out_shape=jax.ShapeDtypeStruct((64, 6, LANES), BF16),
+        in_specs=[
+            pl.BlockSpec(memory_space=pl.ANY),
+            pl.BlockSpec(memory_space=pl.ANY),
+        ],
         scratch_shapes=[
+            pltpu.VMEM((2, 4096), BF16),
+            pltpu.VMEM((32, 8192), BF16),
+            pltpu.SemaphoreType.DMA((17,)),
             pltpu.VMEM((256, 4608), BF16),
             pltpu.VMEM((256, 4608), BF16),
             pltpu.VMEM((256, LANES), F32),
             pltpu.VMEM((264, LANES), F32),
             pltpu.VMEM((64, 8, LANES), F32),
         ],
-        compiler_params=pltpu.CompilerParams(vmem_limit_bytes=16 << 20),
+        compiler_params=pltpu.CompilerParams(vmem_limit_bytes=60 << 20),
         cost_estimate=pl.CostEstimate(
             flops=2 * 256 * 256 * 4608, bytes_accessed=1 << 20, transcendentals=0
         ),
         name="compress",
-    )(echo_rows, replica)
+    )(echoes, replica)
 
 
 def regroup_kernel(turned_ref, out_ref, quads, rows):
@@ -103,12 +133,13 @@
     for core in range(2):
         rows[core, 0:16, :] = jnp.zeros((16, LANES), F32)
         rows[core, 272:288, :] = jnp.zeros((16, LANES), F32)
-        for k in range(4):
-            rows[core, pl.ds(16 + k, 64, stride=4), :] = quads[:, 2 * core + k, :]
-    for y in range(4):
-        for core in range(2):
-            at = 96 * (2 * y + core)
-            out_ref[at : at + 96, :] = rows[core, 64 * y : 64 * y + 96, :].astype(BF16)
+        for at, slot, count in SEGMENTS:
+            for k in range(4):
+                rows[core, pl.ds(16 + 4 * slot + k, count, stride=4), :] = quads[
+                    at : at + count, 2 * core + k, :
+                ]
+    for at, (y, core) in enumerate(LAST):
+        out_ref[96 * at : 96 * at + 96, :] = rows[core, 64 * y : 64 * y + 96, :].astype(BF16)
 
 
 def regroup(turned):
@@ -133,7 +164,9 @@
         block = tap(m)
         for jo in range(1, 4):
             block = jnp.where(group == jo, tap(m - jo), block)
-        table[pl.ds(128 * (m // 4) + m % 4, 32, stride=4), :] = block
+        for part in range(2):
+            at = 128 * (m // 4) + 2 * (m % 4) + part
+            table[pl.ds(at, 16, stride=8), :] = block[16 * part : 16 * part + 16, :]
     out_ref[...] = table[...].astype(BF16)
 
 
@@ -176,10 +209,10 @@
     quads[...] = turned_ref[...].astype(F32)
     slot = lax.broadcasted_iota(jnp.int32, (24, LANES), 0)
     for core in range(2):
-        pulse = 8 * slot + 4 * core + lane_ids(24) % 4
+        pulse = 8 * slot + 4 * core + lane_ids(24) // 2 % 4
         halves = []
         for y in range(4):
-            at = 96 * (2 * y + core)
+            at = 96 * LAST.index((y, core))
             quad = [quads[pl.ds(at + k, 24, stride=4), :] for k in range(4)]
             halves.append(migrate(quad, info_ref, pulse))
         for half in range(2):
@@ -227,12 +260,11 @@
 
 
 def filter_table(recon_filters):
-    by_tap = recon_filters.reshape(16, 4, 4, 2, 64).transpose(4, 1, 2, 3, 0)
-    real, imag = by_tap[:, :, :, 0], by_tap[:, :, :, 1]
-    from_real = jnp.stack([real, imag], -1).reshape(64, 4, 1, 4, 32)
-    from_imag = jnp.stack([-imag, real], -1).reshape(64, 4, 1, 4, 32)
-    table = jnp.concatenate([from_real, from_imag], 2).reshape(64, 32, 32)
-    return jnp.tile(table, (1, 1, 4))
+    real = recon_filters[:, :, 0].transpose(2, 1, 0)
+    imag = recon_filters[:, :, 1].transpose(2, 1, 0)
+    from_real = jnp.stack([real, imag], -1).reshape(64, 16, 32)
+    from_imag = jnp.stack([-imag, real], -1).reshape(64, 16, 32)
+    return jnp.tile(jnp.concatenate([from_real, from_imag], 1), (1, 1, 4))
 
 
 def bin_info(span_offset, span_width, aperture_edges):
@@ -244,14 +276,19 @@
 
 
 def body(echoes, replica, recon_filters, span_offset, span_width, aperture_edges):
-    echo_rows = echoes.transpose(2, 0, 1, 3).reshape(2, 16, 8192)
-    chunks = compress(echo_rows, replica)
-    turned = lax.all_to_all(chunks, "slot", 0, 0, tiled=True)
+    chunks = compress(echoes, replica)
+    order = [slot + i for _, slot, count in SEGMENTS for i in range(count)]
+    turned = lax.all_to_all(chunks, "slot", 0, 0, tiled=True, axis_index_groups=[order])
     info = bin_info(span_offset, span_width, aperture_edges)
     band_matrix = bands(filter_table(recon_filters))
     windows = regroup(turned)
     gathered = lax.all_to_all(
-        windows.reshape(8, 96, LANES), ("chan", "core"), 0, 0, tiled=True
+        windows.reshape(8, 96, LANES),
+        ("chan", "core"),
+        0,
+        0,
+        tiled=True,
+        axis_index_groups=[[2 * y + core for y, core in LAST]],
     )
     image = azimuth(gathered.reshape(768, LANES), info, band_matrix)
     return image.reshape(16, 2, 8, LANES)

time: 53.1 us -> 45.8 us (0.86)
  waiting for transfers between devices: 16.5 us -> 7.14 us
  starting transfers between devices: 27 us -> 29.2 us
  local copies, waits for them, and re-layouts: 4.2 us -> 2.89 us
  Pallas kernels: 4.73 us -> 5.95 us
    all_to_all x1, waiting for transfers between devices: 12.9 us -> 6.1 us  [body(): lax.all_to_all(chunks, 'slot', 0, 0, tiled=True, axis_index_groups=[order])]
    all_to_all x1, starting transfers between devices: 19.2 us -> 22 us  [body(): lax.all_to_all(chunks, 'slot', 0, 0, tiled=True, axis_index_groups=[order])]
    all_to_all x1, waiting for transfers between devices: 3.67 us -> 1.04 us  [body(): lax.all_to_all(windows.reshape(8, 96, LANES), ('chan', 'core'), 0, 0, til...]
    reshape x1 -> x0, local copies, waits for them, and re-layouts: 1.35 us -> none  [body(): echo_rows = echoes.transpose(2, 0, 1, 3).reshape(2, 16, 8192)]
    pallas_call x1, Pallas kernels: 1.94 us -> 3.1 us  [compress(): pl.pallas_call(compress_kernel, out_shape=jax.ShapeDtypeStruct((64, 6, LA...]
    all_to_all x1, starting transfers between devices: 7.81 us -> 7.19 us  [body(): lax.all_to_all(windows.reshape(8, 96, LANES), ('chan', 'core'), 0, 0, til...]
    unnamed x11 -> x8, local copies, waits for them, and re-layouts: 1.39 us -> 1.34 us
  transfers between devices with their start and end apart: 2 -> 2, of which waited for: 2 -> 2; matrix products, arithmetic and copies ran while one was open for 3% -> 4% of each run, Pallas kernels for 0% -> 1%
where the time goes in v3:
time: 45.8 us; the launch traced here: 45.5 us
  starting transfers between devices  29.2 us (64%)
  waiting for transfers between devices  7.14 us (16%)
  Pallas kernels  5.95 us (13%)
  local copies, waits for them, and re-layouts  2.89 us (6%)
    all_to_all x1, starting transfers between devices, body(): lax.all_to_all(chunks, 'slot', 0, 0, tiled=True, axis_index_groups=[order])  22 us
    all_to_all x1, starting transfers between devices, body(): lax.all_to_all(windows.reshape(8, 96, LANES), ('chan', 'core'), 0, 0, til...  7.19 us
    all_to_all x1, waiting for transfers between devices, body(): lax.all_to_all(chunks, 'slot', 0, 0, tiled=True, axis_index_groups=[order])  6.1 us
    pallas_call x1, Pallas kernels, compress(): pl.pallas_call(compress_kernel, out_shape=jax.ShapeDtypeStruct((64, 6, LA...  3.1 us
    pallas_call x1, Pallas kernels, azimuth(): pl.pallas_call(azimuth_kernel, out_shape=jax.ShapeDtypeStruct((256, LANES...  1.77 us
    unnamed x8, local copies, waits for them, and re-layouts  1.34 us
    all_to_all x1, waiting for transfers between devices, body(): lax.all_to_all(windows.reshape(8, 96, LANES), ('chan', 'core'), 0, 0, til...  1.04 us
    another operation x2, local copies, waits for them, and re-layouts, filter_table(): return jnp.tile(jnp.concatenate([from_real, from_imag], 1), (1, 1, 4))  0.99 us
  transfers between devices with their start and end apart: 2, of which 2 were waited for; matrix products, arithmetic and copies ran while one was open for 4% of the time, Pallas kernels for 1%

profile of v3, /device:TPU:1, one launch (start us, length us, event | category | flops | bytes accessed | tf_op | source)
XLA Modules:
  0.0 45.5 jit_solution(2440483611134552307)
XLA Ops:
  0.0 3.1 %compress.1 = bf16[64,6,128]{2,1,0:T(8,128)(2,1)} custom-call(bf16[4,4,2,8192]{3,2,1,0:T(2,128)(2,1)} %echo_ref.1, bf16[2,4096]{1,0:T(2,128)(2,1)} %replica_hbm.1), custom_call_target="tpu_custom_call" | custom-call | flops 603979776 | bytes 1048576 | tf_op jit(solution)/shard_map/compress/pallas_call | solution.py:106
  3.1 0.0 copy-start
  3.1 22.0 %all-to-all-start = ((bf16[64,6,128]{2,1,0:T(8,128)(2,1)}), bf16[64,6,128]{2,1,0:T(8,128)(2,1)S(1)}, u32[]{:S(2)}, u32[]{:S(2)}) async-start(bf16[64,6,128]{2,1,0:T(8,128)(2,1)} %compress.1), calls=%async_computation | async-start | bytes 262144 | tf_op jit(solution)/shard_map/all_to_all | solution.py:281
  25.2 0.0 copy-done
  25.2 0.2 fusion.1
  25.4 0.1 pad_maximum_fusion.1
  25.5 0.0 copy-start.1
  25.5 0.7 %copy-done.1 = s32[2,8]{1,0:T(2,128)S(1)} copy-done((s32[2,8]{1,0:T(2,128)S(1)}, s32[2,8]{1,0:T(2,128)}, u32[]{:S(2)}) %copy-start.1) | copy-done | bytes 88
  26.2 6.1 %all-to-all-done.turned_ref = bf16[64,6,128]{2,1,0:T(8,128)(2,1)S(1)} async-done(((bf16[64,6,128]{2,1,0:T(8,128)(2,1)}), bf16[64,6,128]{2,1,0:T(8,128)(2,1)S(1)}, u32[]{:S(2)}, u32[]{:S(2)}) %all-to-all-start) | async-done | bytes 98336 | tf_op jit(solution)/shard_map/all_to_all | solution.py:281
  32.3 0.8 %regroup.1 = bf16[768,128]{1,0:T(8,128)(2,1)} custom-call(bf16[64,6,128]{2,1,0:T(8,128)(2,1)S(1)} %all-to-all-done.turned_ref), custom_call_target="tpu_custom_call" | custom-call | flops 262144 | bytes 262144 | tf_op jit(solution)/shard_map/regroup/pallas_call | solution.py:146
  33.2 7.2 %all-to-all-start.1 = ((bf16[8,96,128]{2,1,0:T(8,128)(2,1)}), bf16[8,96,128]{2,1,0:T(8,128)(2,1)S(1)}, u32[]{:S(2)}, u32[]{:S(2)}) async-start(bf16[8,96,128]{2,1,0:T(8,128)(2,1)} %bitcast), calls=%async_computation.1 | async-start | bytes 393216 | tf_op jit(solution)/shard_map/all_to_all | solution.py:285
  40.4 0.1 pad_maximum_fusion
  40.4 0.1 copy.12
  40.5 0.2 tile.4
  40.7 0.8 %copy.13.filter_ref = bf16[64,32,128]{2,1,0:T(8,128)(2,1)S(1)} copy(bf16[64,32,128]{0,2,1:T(8,128)(2,1)S(1)} %bitcast.26) | data formatting | bytes 1048576 | tf_op jit(solution)/shard_map/tile | solution.py:267
  41.5 0.0 copy-start.2
  41.5 0.0 copy-start.3
  41.6 0.6 %copy-done.2 = s32[8]{0:T(128)S(1)} copy-done((s32[8]{0:T(128)S(1)}, s32[8]{0:T(128)}, u32[]{:S(2)}) %copy-start.2) | copy-done | bytes 56
  42.2 0.0 copy-done.3
  42.2 0.1 reshape.27
  42.3 0.1 broadcast_in_dim.3
  42.4 0.1 reshape.28.info_ref
  42.5 0.2 bands.1.bands_ref
  42.7 1.0 %all-to-all-done.1 = bf16[8,96,128]{2,1,0:T(8,128)(2,1)S(1)} async-done(((bf16[8,96,128]{2,1,0:T(8,128)(2,1)}), bf16[8,96,128]{2,1,0:T(8,128)(2,1)S(1)}, u32[]{:S(2)}, u32[]{:S(2)}) %all-to-all-start.1) | async-done | bytes 196640 | tf_op jit(solution)/shard_map/all_to_all | solution.py:285
  43.7 1.8 %azimuth.1 = bf16[256,128]{1,0:T(8,128)(2,1)} custom-call(bf16[768,128]{1,0:T(8,128)(2,1)S(1)} %bitcast.25, s32[8,128]{1,0:T(8,128)S(1)} %reshape.28.info_ref, bf16[2304,128]{1,0:T(8,128)(2,1)S(1)} %bands.1.bands_ref), custom_call_target="tpu_custom_call" | custom-call | flops 150994944 | bytes 1048576 | tf_op jit(solution)/shard_map/azimuth/pallas_call | solution.py:243
  (6 shorter events, 0.1 us)
Async XLA Ops:
  3.1 22.1 %copy-start = (bf16[16,16,2,64]{3,2,1,0:T(2,128)(2,1)S(1)}, bf16[16,16,2,64]{3,2,1,0:T(2,128)(2,1)}, u32[]{:S(2)}) copy-start(bf16[16,16,2,64]{3,2,1,0:T(2,128)(2,1)} %param.8) | copy-start | bytes 196612
  3.1 29.2 %all-to-all-start = ((bf16[64,6,128]{2,1,0:T(8,128)(2,1)}), bf16[64,6,128]{2,1,0:T(8,128)(2,1)S(1)}, u32[]{:S(2)}, u32[]{:S(2)}) async-start(bf16[64,6,128]{2,1,0:T(8,128)(2,1)} %compress.1), calls=%async_computation | async-start | bytes 262144 | tf_op jit(solution)/shard_map/all_to_all | solution.py:281
  25.5 0.7 %copy-start.1 = (s32[2,8]{1,0:T(2,128)S(1)}, s32[2,8]{1,0:T(2,128)}, u32[]{:S(2)}) copy-start(s32[2,8]{1,0:T(2,128)} %param.11) | copy-start | bytes 196
  33.2 10.6 %all-to-all-start.1 = ((bf16[8,96,128]{2,1,0:T(8,128)(2,1)}), bf16[8,96,128]{2,1,0:T(8,128)(2,1)S(1)}, u32[]{:S(2)}, u32[]{:S(2)}) async-start(bf16[8,96,128]{2,1,0:T(8,128)(2,1)} %bitcast), calls=%async_computation.1 | async-start | bytes 393216 | tf_op jit(solution)/shard_map/all_to_all | solution.py:285
  41.5 0.7 %copy-start.2 = (s32[8]{0:T(128)S(1)}, s32[8]{0:T(128)}, u32[]{:S(2)}) copy-start(s32[8]{0:T(128)} %param.10) | copy-start | bytes 100
  41.5 0.7 %copy-start.3 = (s32[8]{0:T(128)S(1)}, s32[8]{0:T(128)}, u32[]{:S(2)}) copy-start(s32[8]{0:T(128)} %param.9) | copy-start | bytes 100

commit v4 on v3

--- a/solution.py
+++ b/solution.py
@@ -107,8 +107,8 @@
         compress_kernel,
         out_shape=jax.ShapeDtypeStruct((64, 6, LANES), BF16),
         in_specs=[
-            pl.BlockSpec(memory_space=pl.ANY),
-            pl.BlockSpec(memory_space=pl.ANY),
+            pl.BlockSpec(memory_space=pltpu.HBM),
+            pl.BlockSpec(memory_space=pltpu.HBM),
         ],
         scratch_shapes=[
             pltpu.VMEM((2, 4096), BF16),
@@ -120,12 +120,15 @@
             pltpu.VMEM((264, LANES), F32),
             pltpu.VMEM((64, 8, LANES), F32),
         ],
-        compiler_params=pltpu.CompilerParams(vmem_limit_bytes=60 << 20),
+        compiler_params=pltpu.CompilerParams(vmem_limit_bytes=16 << 20),
         cost_estimate=pl.CostEstimate(
             flops=2 * 256 * 256 * 4608, bytes_accessed=1 << 20, transcendentals=0
         ),
         name="compress",
-    )(echoes, replica)
+    )(
+        pltpu.with_memory_space_constraint(echoes, pltpu.HBM),
+        pltpu.with_memory_space_constraint(replica, pltpu.HBM),
+    )
 
 
 def regroup_kernel(turned_ref, out_ref, quads, rows):
@@ -153,12 +156,18 @@
     )(turned)
 
 
-def bands_kernel(filter_ref, out_ref, table):
+def bands_kernel(
+    filter_ref, offset_ref, width_ref, edges_ref, out_ref, info_ref, spread, table
+):
     group = lane_ids(32) // 32
     zero = jnp.zeros((32, LANES), F32)
+    repeat = lane_ids(32) % 32 == lax.broadcasted_iota(jnp.int32, (32, LANES), 0)
+    spread[...] = jnp.dot(
+        filter_ref[...].reshape(2048, 32), repeat.astype(BF16), preferred_element_type=F32
+    )
 
     def tap(t):
-        return filter_ref[t].astype(F32) if 0 <= t < 64 else zero
+        return spread[32 * t : 32 * t + 32, :] if 0 <= t < 64 else zero
 
     for m in range(72):
         block = tap(m)
@@ -169,16 +178,40 @@
             table[pl.ds(at, 16, stride=8), :] = block[16 * part : 16 * part + 16, :]
     out_ref[...] = table[...].astype(BF16)
 
-
-def bands(filter_table):
+    def spread_bins(value):
+        rows = []
+        for half in range(2):
+            row = jnp.full((1, LANES), value(4 * half), jnp.int32)
+            for il in range(1, 4):
+                row = jnp.where(group[:1] == il, value(4 * half + il), row)
+            rows.append(row)
+        return rows
+
+    values = (
+        lambda i: offset_ref[i],
+        lambda i: width_ref[i],
+        lambda i: edges_ref[0, i],
+        lambda i: 512 - edges_ref[1, i],
+    )
+    for kind, value in enumerate(values):
+        for half, row in enumerate(spread_bins(value)):
+            info_ref[2 * kind + half : 2 * kind + half + 1, :] = row
+
+
+def bands(filter_table, span_offset, span_width, aperture_edges):
+    scalars = pl.BlockSpec(memory_space=pltpu.SMEM)
     return pl.pallas_call(
         bands_kernel,
-        out_shape=jax.ShapeDtypeStruct((2304, LANES), BF16),
-        scratch_shapes=[pltpu.VMEM((2304, LANES), F32)],
+        out_shape=(
+            jax.ShapeDtypeStruct((2304, LANES), BF16),
+            jax.ShapeDtypeStruct((8, LANES), jnp.int32),
+        ),
+        in_specs=[pl.BlockSpec(memory_space=pltpu.VMEM), scalars, scalars, scalars],
+        scratch_shapes=[pltpu.VMEM((2048, LANES), F32), pltpu.VMEM((2304, LANES), F32)],
         compiler_params=pltpu.CompilerParams(vmem_limit_bytes=8 << 20),
         cost_estimate=pl.CostEstimate(flops=1 << 20, bytes_accessed=1 << 20, transcendentals=0),
         name="bands",
-    )(filter_table)
+    )(filter_table, span_offset, span_width, aperture_edges)
 
 
 def migrate(quad, info_ref, pulse):
@@ -208,8 +241,9 @@
 ):
     quads[...] = turned_ref[...].astype(F32)
     slot = lax.broadcasted_iota(jnp.int32, (24, LANES), 0)
+    origin = 128 * lax.axis_index("chan") - 32
     for core in range(2):
-        pulse = 8 * slot + 4 * core + lane_ids(24) // 2 % 4
+        pulse = origin + 8 * slot + 4 * core + lane_ids(24) // 2 % 4
         halves = []
         for y in range(4):
             at = 96 * LAST.index((y, core))
@@ -264,24 +298,20 @@
     imag = recon_filters[:, :, 1].transpose(2, 1, 0)
     from_real = jnp.stack([real, imag], -1).reshape(64, 16, 32)
     from_imag = jnp.stack([-imag, real], -1).reshape(64, 16, 32)
-    return jnp.tile(jnp.concatenate([from_real, from_imag], 1), (1, 1, 4))
-
-
-def bin_info(span_offset, span_width, aperture_edges):
-    origin = 128 * lax.axis_index("chan") - 32
-    info = jnp.stack(
-        [span_offset, span_width, aperture_edges[0] - origin, 512 - aperture_edges[1] - origin], 0
-    )
-    return jnp.repeat(info.reshape(8, 4), 32, axis=1)
+    return jnp.concatenate([from_real, from_imag], 1)
 
 
 def body(echoes, replica, recon_filters, span_offset, span_width, aperture_edges):
     chunks = compress(echoes, replica)
     order = [slot + i for _, slot, count in SEGMENTS for i in range(count)]
     turned = lax.all_to_all(chunks, "slot", 0, 0, tiled=True, axis_index_groups=[order])
-    info = bin_info(span_offset, span_width, aperture_edges)
-    band_matrix = bands(filter_table(recon_filters))
     windows = regroup(turned)
+    windows, recon_filters, span_offset, span_width, aperture_edges = lax.optimization_barrier(
+        (windows, recon_filters, span_offset, span_width, aperture_edges)
+    )
+    band_matrix, info = bands(
+        filter_table(recon_filters), span_offset, span_width, aperture_edges
+    )
     gathered = lax.all_to_all(
         windows.reshape(8, 96, LANES),
         ("chan", "core"),

time: 45.8 us -> 44.9 us (0.980)
  blocking collectives: 0 us -> 28.8 us
  starting transfers between devices: 29.2 us -> 7.2 us
  waiting for transfers between devices: 7.14 us -> 1.04 us
  local copies, waits for them, and re-layouts: 2.89 us -> 1.24 us
    all_to_all x0 -> x1, blocking collectives: none -> 28.8 us  [body(): lax.all_to_all(chunks, 'slot', 0, 0, tiled=True, axis_index_groups=[order])]
    all_to_all x1 -> x0, starting transfers between devices: 22 us -> none  [body(): lax.all_to_all(chunks, 'slot', 0, 0, tiled=True, axis_index_groups=[order])]
    all_to_all x1 -> x0, waiting for transfers between devices: 6.1 us -> none  [body(): lax.all_to_all(chunks, 'slot', 0, 0, tiled=True, axis_index_groups=[order])]
    another operation x2 -> x0, local copies, waits for them, and re-layouts: 0.99 us -> none  [filter_table(): return jnp.tile(jnp.concatenate([from_real, from_imag], 1), (1, 1, 4))]
    pallas_call x1, Pallas kernels: 0.23 us -> 0.96 us  [bands(): pl.pallas_call(bands_kernel, out_shape=(jax.ShapeDtypeStruct((2304, LANES...]
    unnamed x8, local copies, waits for them, and re-layouts: 1.34 us -> 0.62 us
    pallas_call x1, Pallas kernels: 3.1 us -> 2.48 us  [compress(): pl.pallas_call(compress_kernel, out_shape=jax.ShapeDtypeStruct((64, 6, LA...]
  transfers between devices with their start and end apart: 2 -> 1, of which waited for: 2 -> 1; matrix products, arithmetic and copies ran while one was open for 4% -> 2% of each run, Pallas kernels for 1% -> 2%
where the time goes in v4:
time: 44.9 us; the launch traced here: 44.6 us
  blocking collectives  28.8 us (64%)
  starting transfers between devices  7.2 us (16%)
  Pallas kernels  6.03 us (13%)
  local copies, waits for them, and re-layouts  1.24 us (3%)
  waiting for transfers between devices  1.04 us (2%)
    all_to_all x1, blocking collectives, body(): lax.all_to_all(chunks, 'slot', 0, 0, tiled=True, axis_index_groups=[order])  28.8 us
    all_to_all x1, starting transfers between devices, body(): lax.all_to_all(windows.reshape(8, 96, LANES), ('chan', 'core'), 0, 0, til...  7.2 us
    pallas_call x1, Pallas kernels, compress(): pl.pallas_call(compress_kernel, out_shape=jax.ShapeDtypeStruct((64, 6, LA...  2.48 us
    pallas_call x1, Pallas kernels, azimuth(): pl.pallas_call(azimuth_kernel, out_shape=jax.ShapeDtypeStruct((256, LANES...  1.76 us
    all_to_all x1, waiting for transfers between devices, body(): lax.all_to_all(windows.reshape(8, 96, LANES), ('chan', 'core'), 0, 0, til...  1.04 us
    pallas_call x1, Pallas kernels, bands(): pl.pallas_call(bands_kernel, out_shape=(jax.ShapeDtypeStruct((2304, LANES...  0.96 us
  transfers between devices with their start and end apart: 1, of which 1 were waited for; matrix products, arithmetic and copies ran while one was open for 2% of the time, Pallas kernels for 2%

profile of v4, /device:TPU:1, one launch (start us, length us, event | category | flops | bytes accessed | tf_op | source)
XLA Modules:
  0.0 44.6 jit_solution(514761413269708767)
XLA Ops:
  0.0 2.5 %compress.1 = bf16[64,6,128]{2,1,0:T(8,128)(2,1)S(1)} custom-call(bf16[4,4,2,8192]{3,2,1,0:T(2,128)(2,1)} %echo_ref.1, bf16[2,4096]{1,0:T(2,128)(2,1)} %replica_hbm.1), custom_call_target="tpu_custom_call" | custom-call | flops 603979776 | bytes 1048576 | tf_op jit(solution)/shard_map/compress/pallas_call | solution.py:106
  2.5 28.8 %all_to_all.10.turned_ref = bf16[64,6,128]{2,1,0:T(8,128)(2,1)S(1)} all-to-all(bf16[64,6,128]{2,1,0:T(8,128)(2,1)S(1)} %compress.1), channel_id=1, replica_groups={{328,336,344,352,360,368,376,384,392,400,408,416,424,432,440,448,456,46..., dimensions={0} | all-to-all | bytes 196608 | tf_op jit(solution)/shard_map/all_to_all | solution.py:307
  31.3 0.0 copy-start.3
  31.3 0.8 %regroup.1 = bf16[768,128]{1,0:T(8,128)(2,1)} custom-call(bf16[64,6,128]{2,1,0:T(8,128)(2,1)S(1)} %all_to_all.10.turned_ref), custom_call_target="tpu_custom_call" | custom-call | flops 262144 | bytes 262144 | tf_op jit(solution)/shard_map/regroup/pallas_call | solution.py:149
  32.2 0.1 copy-done.3
  32.3 7.2 %all-to-all-start.1 = ((bf16[8,96,128]{2,1,0:T(8,128)(2,1)}), bf16[8,96,128]{2,1,0:T(8,128)(2,1)S(1)}, u32[]{:S(2)}, u32[]{:S(2)}) async-start(bf16[8,96,128]{2,1,0:T(8,128)(2,1)} %bitcast), calls=%async_computation.1 | async-start | bytes 393216 | tf_op jit(solution)/shard_map/all_to_all | solution.py:315
  39.5 0.1 pad_maximum_fusion.1
  39.6 0.3 copy.14
  39.9 0.3 copy.15
  40.2 0.0 copy-start
  40.2 0.0 copy-start.1
  40.2 0.0 copy-start.2
  40.2 0.1 pad_maximum_fusion.filter_ref
  40.3 0.5 %copy-done = s32[2,8]{1,0:T(2,128)S(1)} copy-done((s32[2,8]{1,0:T(2,128)S(1)}, s32[2,8]{1,0:T(2,128)}, u32[]{:S(2)}) %copy-start) | copy-done | bytes 88
  40.9 0.0 copy-done.1
  40.9 0.0 copy-done.2
  40.9 1.0 %bands.1 = (bf16[2304,128]{1,0:T(8,128)(2,1)S(1)}, s32[8,128]{1,0:T(8,128)S(1)}) custom-call(bf16[64,32,32]{2,1,0:T(8,128)(2,1)S(1)} %pad_maximum_fusion.filter_ref, s32[8]{0:T(128)S(1)} %copy-done.1, s32[8]{0:T(128)S(1)} %copy-done.2, s32[2,8]{1,0:T(2,128)S(1)} %copy-done), custom_call_target="tpu_custom_call" | custom-call | flops 1048576 | bytes 1048576 | tf_op jit(solution)/shard_map/bands/pallas_call | solution.py:203
  41.8 1.0 %all-to-all-done.1 = bf16[8,96,128]{2,1,0:T(8,128)(2,1)S(1)} async-done(((bf16[8,96,128]{2,1,0:T(8,128)(2,1)}), bf16[8,96,128]{2,1,0:T(8,128)(2,1)S(1)}, u32[]{:S(2)}, u32[]{:S(2)}) %all-to-all-start.1) | async-done | bytes 196640 | tf_op jit(solution)/shard_map/all_to_all | solution.py:315
  42.9 1.8 %azimuth.1 = bf16[256,128]{1,0:T(8,128)(2,1)} custom-call(bf16[768,128]{1,0:T(8,128)(2,1)S(1)} %bitcast.22, s32[8,128]{1,0:T(8,128)S(1)} %get-tuple-element.17.info_ref, bf16[2304,128]{1,0:T(8,128)(2,1)S(1)} %get-tuple-element.18.bands_ref), custom_call_target="tpu_custom_call" | custom-call | flops 150994944 | bytes 1048576 | tf_op jit(solution)/shard_map/azimuth/pallas_call | solution.py:277
  (5 shorter events, 0.1 us)
Async XLA Ops:
  31.3 0.9 %copy-start.3 = (bf16[16,16,2,64]{3,2,1,0:T(2,128)(2,1)S(1)}, bf16[16,16,2,64]{3,2,1,0:T(2,128)(2,1)}, u32[]{:S(2)}) copy-start(bf16[16,16,2,64]{3,2,1,0:T(2,128)(2,1)} %param.8) | copy-start | bytes 196612
  32.3 10.6 %all-to-all-start.1 = ((bf16[8,96,128]{2,1,0:T(8,128)(2,1)}), bf16[8,96,128]{2,1,0:T(8,128)(2,1)S(1)}, u32[]{:S(2)}, u32[]{:S(2)}) async-start(bf16[8,96,128]{2,1,0:T(8,128)(2,1)} %bitcast), calls=%async_computation.1 | async-start | bytes 393216 | tf_op jit(solution)/shard_map/all_to_all | solution.py:315
  40.2 0.7 %copy-start = (s32[2,8]{1,0:T(2,128)S(1)}, s32[2,8]{1,0:T(2,128)}, u32[]{:S(2)}) copy-start(s32[2,8]{1,0:T(2,128)} %edges_ref) | copy-start | bytes 196
  40.2 0.7 %copy-start.1 = (s32[8]{0:T(128)S(1)}, s32[8]{0:T(128)}, u32[]{:S(2)}) copy-start(s32[8]{0:T(128)} %offset_ref) | copy-start | bytes 100
  40.2 0.7 %copy-start.2 = (s32[8]{0:T(128)S(1)}, s32[8]{0:T(128)}, u32[]{:S(2)}) copy-start(s32[8]{0:T(128)} %width_ref) | copy-start | bytes 100

commit v5 on v4

--- a/solution.py
+++ b/solution.py
@@ -11,7 +11,7 @@
 LANES = 128
 NT = (((1,), (1,)), ((), ()))
 FIRST = 41
-LAST = ((2, 0), (2, 1), (3, 0), (3, 1), (0, 0), (0, 1), (1, 0), (1, 1))
+LAST = ((2, 1), (2, 0), (3, 1), (3, 0), (0, 1), (0, 0), (1, 1), (1, 0))
 SEGMENTS = ((0, FIRST, 64 - FIRST), (64 - FIRST, 0, FIRST))
 
 

time: 44.9 us -> 44.3 us (0.987)
  starting transfers between devices: 7.2 us -> 6.24 us
    all_to_all x1, starting transfers between devices: 7.2 us -> 6.24 us  [body(): lax.all_to_all(windows.reshape(8, 96, LANES), ('chan', 'core'), 0, 0, til...]
where the time goes in v5:
time: 44.3 us; the launch traced here: 44 us
  blocking collectives  28.8 us (65%)
  starting transfers between devices  6.24 us (14%)
  Pallas kernels  6.02 us (14%)
  waiting for transfers between devices  1.4 us (3%)
  local copies, waits for them, and re-layouts  1.24 us (3%)
    all_to_all x1, blocking collectives, body(): lax.all_to_all(chunks, 'slot', 0, 0, tiled=True, axis_index_groups=[order])  28.8 us
    all_to_all x1, starting transfers between devices, body(): lax.all_to_all(windows.reshape(8, 96, LANES), ('chan', 'core'), 0, 0, til...  6.24 us
    pallas_call x1, Pallas kernels, compress(): pl.pallas_call(compress_kernel, out_shape=jax.ShapeDtypeStruct((64, 6, LA...  2.48 us
    pallas_call x1, Pallas kernels, azimuth(): pl.pallas_call(azimuth_kernel, out_shape=jax.ShapeDtypeStruct((256, LANES...  1.76 us
    all_to_all x1, waiting for transfers between devices, body(): lax.all_to_all(windows.reshape(8, 96, LANES), ('chan', 'core'), 0, 0, til...  1.4 us
    pallas_call x1, Pallas kernels, bands(): pl.pallas_call(bands_kernel, out_shape=(jax.ShapeDtypeStruct((2304, LANES...  0.95 us
  transfers between devices with their start and end apart: 1, of which 1 were waited for; matrix products, arithmetic and copies ran while one was open for 2% of the time, Pallas kernels for 2%

profile of v5, /device:TPU:1, one launch (start us, length us, event | category | flops | bytes accessed | tf_op | source)
XLA Modules:
  0.0 44.0 jit_solution(18026769756912625599)
XLA Ops:
  0.0 2.5 %compress.1 = bf16[64,6,128]{2,1,0:T(8,128)(2,1)S(1)} custom-call(bf16[4,4,2,8192]{3,2,1,0:T(2,128)(2,1)} %echo_ref.1, bf16[2,4096]{1,0:T(2,128)(2,1)} %replica_hbm.1), custom_call_target="tpu_custom_call" | custom-call | flops 603979776 | bytes 1048576 | tf_op jit(solution)/shard_map/compress/pallas_call | solution.py:106
  2.5 28.8 %all_to_all.10.turned_ref = bf16[64,6,128]{2,1,0:T(8,128)(2,1)S(1)} all-to-all(bf16[64,6,128]{2,1,0:T(8,128)(2,1)S(1)} %compress.1), channel_id=1, replica_groups={{328,336,344,352,360,368,376,384,392,400,408,416,424,432,440,448,456,46..., dimensions={0} | all-to-all | bytes 196608 | tf_op jit(solution)/shard_map/all_to_all | solution.py:307
  31.3 0.0 copy-start.3
  31.3 0.8 %regroup.1 = bf16[768,128]{1,0:T(8,128)(2,1)} custom-call(bf16[64,6,128]{2,1,0:T(8,128)(2,1)S(1)} %all_to_all.10.turned_ref), custom_call_target="tpu_custom_call" | custom-call | flops 262144 | bytes 262144 | tf_op jit(solution)/shard_map/regroup/pallas_call | solution.py:149
  32.2 0.1 copy-done.3
  32.3 6.2 %all-to-all-start.1 = ((bf16[8,96,128]{2,1,0:T(8,128)(2,1)}), bf16[8,96,128]{2,1,0:T(8,128)(2,1)S(1)}, u32[]{:S(2)}, u32[]{:S(2)}) async-start(bf16[8,96,128]{2,1,0:T(8,128)(2,1)} %bitcast), calls=%async_computation.1 | async-start | bytes 393216 | tf_op jit(solution)/shard_map/all_to_all | solution.py:315
  38.5 0.1 pad_maximum_fusion.1
  38.6 0.3 copy.14
  38.9 0.3 copy.15
  39.2 0.0 copy-start
  39.2 0.0 copy-start.1
  39.2 0.0 copy-start.2
  39.2 0.1 pad_maximum_fusion.filter_ref
  39.4 0.5 %copy-done = s32[2,8]{1,0:T(2,128)S(1)} copy-done((s32[2,8]{1,0:T(2,128)S(1)}, s32[2,8]{1,0:T(2,128)}, u32[]{:S(2)}) %copy-start) | copy-done | bytes 88
  39.9 0.0 copy-done.1
  39.9 0.0 copy-done.2
  39.9 0.9 %bands.1 = (bf16[2304,128]{1,0:T(8,128)(2,1)S(1)}, s32[8,128]{1,0:T(8,128)S(1)}) custom-call(bf16[64,32,32]{2,1,0:T(8,128)(2,1)S(1)} %pad_maximum_fusion.filter_ref, s32[8]{0:T(128)S(1)} %copy-done.1, s32[8]{0:T(128)S(1)} %copy-done.2, s32[2,8]{1,0:T(2,128)S(1)} %copy-done), custom_call_target="tpu_custom_call" | custom-call | flops 1048576 | bytes 1048576 | tf_op jit(solution)/shard_map/bands/pallas_call | solution.py:203
  40.9 1.4 %all-to-all-done.1 = bf16[8,96,128]{2,1,0:T(8,128)(2,1)S(1)} async-done(((bf16[8,96,128]{2,1,0:T(8,128)(2,1)}), bf16[8,96,128]{2,1,0:T(8,128)(2,1)S(1)}, u32[]{:S(2)}, u32[]{:S(2)}) %all-to-all-start.1) | async-done | bytes 196640 | tf_op jit(solution)/shard_map/all_to_all | solution.py:315
  42.2 1.8 %azimuth.1 = bf16[256,128]{1,0:T(8,128)(2,1)} custom-call(bf16[768,128]{1,0:T(8,128)(2,1)S(1)} %bitcast.22, s32[8,128]{1,0:T(8,128)S(1)} %get-tuple-element.17.info_ref, bf16[2304,128]{1,0:T(8,128)(2,1)S(1)} %get-tuple-element.18.bands_ref), custom_call_target="tpu_custom_call" | custom-call | flops 150994944 | bytes 1048576 | tf_op jit(solution)/shard_map/azimuth/pallas_call | solution.py:277
  (5 shorter events, 0.1 us)
Async XLA Ops:
  31.3 0.9 %copy-start.3 = (bf16[16,16,2,64]{3,2,1,0:T(2,128)(2,1)S(1)}, bf16[16,16,2,64]{3,2,1,0:T(2,128)(2,1)}, u32[]{:S(2)}) copy-start(bf16[16,16,2,64]{3,2,1,0:T(2,128)(2,1)} %param.8) | copy-start | bytes 196612
  32.3 10.0 %all-to-all-start.1 = ((bf16[8,96,128]{2,1,0:T(8,128)(2,1)}), bf16[8,96,128]{2,1,0:T(8,128)(2,1)S(1)}, u32[]{:S(2)}, u32[]{:S(2)}) async-start(bf16[8,96,128]{2,1,0:T(8,128)(2,1)} %bitcast), calls=%async_computation.1 | async-start | bytes 393216 | tf_op jit(solution)/shard_map/all_to_all | solution.py:315
  39.2 0.7 %copy-start = (s32[2,8]{1,0:T(2,128)S(1)}, s32[2,8]{1,0:T(2,128)}, u32[]{:S(2)}) copy-start(s32[2,8]{1,0:T(2,128)} %edges_ref) | copy-start | bytes 196
  39.2 0.7 %copy-start.1 = (s32[8]{0:T(128)S(1)}, s32[8]{0:T(128)}, u32[]{:S(2)}) copy-start(s32[8]{0:T(128)} %offset_ref) | copy-start | bytes 100
  39.2 0.7 %copy-start.2 = (s32[8]{0:T(128)S(1)}, s32[8]{0:T(128)}, u32[]{:S(2)}) copy-start(s32[8]{0:T(128)} %width_ref) | copy-start | bytes 100

commit v6 on v5

--- a/solution.py
+++ b/solution.py
@@ -10,7 +10,7 @@
 BF16 = jnp.bfloat16
 LANES = 128
 NT = (((1,), (1,)), ((), ()))
-FIRST = 41
+FIRST = 40
 LAST = ((2, 1), (2, 0), (3, 1), (3, 0), (0, 1), (0, 0), (1, 1), (1, 0))
 SEGMENTS = ((0, FIRST, 64 - FIRST), (64 - FIRST, 0, FIRST))
 
@@ -131,29 +131,54 @@
     )
 
 
-def regroup_kernel(turned_ref, out_ref, quads, rows):
+def migrate(quad, info, pulse):
+    rows = quad[0].shape[0]
+    group = lane_ids(rows) // 32
+    shifted = [quad]
+    for f in range(1, 4):
+        rolled = [pltpu.roll(q, LANES - 32 * f, 1) for q in quad]
+        shifted.append([jnp.where(group < 4 - f, rolled[k], rolled[k + 1]) for k in range(3)])
+    halves = []
+    for half in range(2):
+        first = info[half : half + 1, :]
+        width = info[2 + half : 3 + half, :]
+        low = info[4 + half : 5 + half, :]
+        high = info[6 + half : 7 + half, :]
+        total = jnp.zeros((rows, LANES), F32)
+        for step in range(8):
+            inside = (first <= step) & (step < first + width)
+            total = total + jnp.where(inside, shifted[step % 4][half + step // 4], 0.0)
+        total = total * (1.0 / width.astype(F32))
+        halves.append(jnp.where((pulse >= low) & (pulse < high), total, 0.0))
+    return halves
+
+
+def regroup_kernel(turned_ref, info_ref, other_ref, out_ref, quads, rows):
     quads[:, 0:6, :] = turned_ref[...].astype(F32)
+    here = lax.axis_index("core")
+    slot = (lax.broadcasted_iota(jnp.int32, (64, LANES), 0) + FIRST) % 64
+    pulse = 8 * slot + 4 * here + lane_ids(64) // 2 % 4
     for core in range(2):
-        rows[core, 0:16, :] = jnp.zeros((16, LANES), F32)
-        rows[core, 272:288, :] = jnp.zeros((16, LANES), F32)
-        for at, slot, count in SEGMENTS:
-            for k in range(4):
-                rows[core, pl.ds(16 + 4 * slot + k, count, stride=4), :] = quads[
-                    at : at + count, 2 * core + k, :
-                ]
+        info = jnp.where(here == core, info_ref[...], other_ref[...])
+        rows[core, 0:8, :] = jnp.zeros((8, LANES), F32)
+        rows[core, 136:144, :] = jnp.zeros((8, LANES), F32)
+        quad = [quads[:, 2 * core + k, :] for k in range(4)]
+        for half, bins in enumerate(migrate(quad, info, pulse)):
+            for at, first, count in SEGMENTS:
+                rows[core, pl.ds(8 + 2 * first + half, count, stride=2), :] = bins[at : at + count]
     for at, (y, core) in enumerate(LAST):
-        out_ref[96 * at : 96 * at + 96, :] = rows[core, 64 * y : 64 * y + 96, :].astype(BF16)
-
-
-def regroup(turned):
+        out_ref[48 * at : 48 * at + 48, :] = rows[core, 32 * y : 32 * y + 48, :].astype(BF16)
+
+
+def regroup(turned, info, other):
     return pl.pallas_call(
         regroup_kernel,
-        out_shape=jax.ShapeDtypeStruct((768, LANES), BF16),
-        scratch_shapes=[pltpu.VMEM((64, 8, LANES), F32), pltpu.VMEM((2, 288, LANES), F32)],
+        out_shape=jax.ShapeDtypeStruct((384, LANES), BF16),
+        scratch_shapes=[pltpu.VMEM((64, 8, LANES), F32), pltpu.VMEM((2, 144, LANES), F32)],
         compiler_params=pltpu.CompilerParams(vmem_limit_bytes=8 << 20),
-        cost_estimate=pl.CostEstimate(flops=1 << 18, bytes_accessed=1 << 18, transcendentals=0),
+        cost_estimate=pl.CostEstimate(flops=1 << 20, bytes_accessed=1 << 18, transcendentals=0),
         name="regroup",
-    )(turned)
+    )(turned, info, other)
 
 
 def bands_kernel(
@@ -214,43 +239,14 @@
     )(filter_table, span_offset, span_width, aperture_edges)
 
 
-def migrate(quad, info_ref, pulse):
-    rows = quad[0].shape[0]
-    group = lane_ids(rows) // 32
-    shifted = [quad]
-    for f in range(1, 4):
-        rolled = [pltpu.roll(q, LANES - 32 * f, 1) for q in quad]
-        shifted.append([jnp.where(group < 4 - f, rolled[k], rolled[k + 1]) for k in range(3)])
-    halves = []
-    for half in range(2):
-        first = info_ref[half : half + 1, :]
-        width = info_ref[2 + half : 3 + half, :]
-        low = info_ref[4 + half : 5 + half, :]
-        high = info_ref[6 + half : 7 + half, :]
-        total = jnp.zeros((rows, LANES), F32)
-        for step in range(8):
-            inside = (first <= step) & (step < first + width)
-            total = total + jnp.where(inside, shifted[step % 4][half + step // 4], 0.0)
-        total = total * (1.0 / width.astype(F32))
-        halves.append(jnp.where((pulse >= low) & (pulse < high), total, 0.0))
-    return halves
-
-
-def azimuth_kernel(
-    turned_ref, info_ref, bands_ref, out_ref, quads, field, pair, result, planes, final
-):
-    quads[...] = turned_ref[...].astype(F32)
-    slot = lax.broadcasted_iota(jnp.int32, (24, LANES), 0)
-    origin = 128 * lax.axis_index("chan") - 32
+def azimuth_kernel(turned_ref, bands_ref, out_ref, bins, field, pair, result, planes, final):
+    bins[...] = turned_ref[...].astype(F32)
     for core in range(2):
-        pulse = origin + 8 * slot + 4 * core + lane_ids(24) // 2 % 4
-        halves = []
-        for y in range(4):
-            at = 96 * LAST.index((y, core))
-            quad = [quads[pl.ds(at + k, 24, stride=4), :] for k in range(4)]
-            halves.append(migrate(quad, info_ref, pulse))
         for half in range(2):
-            for il, piece in enumerate(swap_blocks([h[half] for h in halves], 32)):
+            arrays = [
+                bins[pl.ds(48 * LAST.index((y, core)) + half, 24, stride=2), :] for y in range(4)
+            ]
+            for il, piece in enumerate(swap_blocks(arrays, 32)):
                 field[pl.ds(8 * core + 4 * half + il, 24, stride=16), :] = piece
     field[384:392, :] = jnp.zeros((8, LANES), F32)
     pair[:, :LANES] = field[0:384, :].astype(BF16)
@@ -273,12 +269,12 @@
     out_ref[...] = final[...].astype(BF16)
 
 
-def azimuth(turned, info, band_matrix):
+def azimuth(turned, band_matrix):
     return pl.pallas_call(
         azimuth_kernel,
         out_shape=jax.ShapeDtypeStruct((256, LANES), BF16),
         scratch_shapes=[
-            pltpu.VMEM((768, LANES), F32),
+            pltpu.VMEM((384, LANES), F32),
             pltpu.VMEM((392, LANES), F32),
             pltpu.VMEM((384, 256), BF16),
             pltpu.VMEM((256, LANES), F32),
@@ -290,7 +286,7 @@
         ),
         compiler_params=pltpu.CompilerParams(vmem_limit_bytes=8 << 20),
         name="azimuth",
-    )(turned, info, band_matrix)
+    )(turned, band_matrix)
 
 
 def filter_table(recon_filters):
@@ -305,22 +301,23 @@
     chunks = compress(echoes, replica)
     order = [slot + i for _, slot, count in SEGMENTS for i in range(count)]
     turned = lax.all_to_all(chunks, "slot", 0, 0, tiled=True, axis_index_groups=[order])
-    windows = regroup(turned)
-    windows, recon_filters, span_offset, span_width, aperture_edges = lax.optimization_barrier(
-        (windows, recon_filters, span_offset, span_width, aperture_edges)
+    _, recon_filters, span_offset, span_width, aperture_edges = lax.optimization_barrier(
+        (chunks, recon_filters, span_offset, span_width, aperture_edges)
     )
     band_matrix, info = bands(
         filter_table(recon_filters), span_offset, span_width, aperture_edges
     )
+    other = lax.ppermute(info, "core", [(0, 1), (1, 0)])
+    windows = regroup(turned, info, other)
     gathered = lax.all_to_all(
-        windows.reshape(8, 96, LANES),
+        windows.reshape(8, 48, LANES),
         ("chan", "core"),
         0,
         0,
         tiled=True,
         axis_index_groups=[[2 * y + core for y, core in LAST]],
     )
-    image = azimuth(gathered.reshape(768, LANES), info, band_matrix)
+    image = azimuth(gathered.reshape(384, LANES), band_matrix)
     return image.reshape(16, 2, 8, LANES)
 
 

time: 44.3 us -> 43.1 us (0.973)
  blocking collectives: 28.8 us -> 8.51 us
  starting transfers between devices: 6.24 us -> 26.1 us
  waiting for transfers between devices: 1.4 us -> 0.8 us
    all_to_all x1, blocking collectives: 28.8 us -> 8.51 us  [body(): lax.all_to_all(windows.reshape(8, 48, LANES), ('chan', 'core'), 0, 0, til...]
    all_to_all x1, starting transfers between devices: 6.24 us -> 22.9 us  [body(): lax.all_to_all(chunks, 'slot', 0, 0, tiled=True, axis_index_groups=[order])]
    ppermute x0 -> x1, starting transfers between devices: none -> 3.15 us  [body(): other = lax.ppermute(info, 'core', [(0, 1), (1, 0)])]
    all_to_all x1, waiting for transfers between devices: 1.4 us -> 0.01 us  [body(): lax.all_to_all(chunks, 'slot', 0, 0, tiled=True, axis_index_groups=[order])]
    ppermute x0 -> x1, waiting for transfers between devices: none -> 0.8 us  [body(): other = lax.ppermute(info, 'core', [(0, 1), (1, 0)])]
    pallas_call x1, Pallas kernels: 2.48 us -> 3.11 us  [compress(): pl.pallas_call(compress_kernel, out_shape=jax.ShapeDtypeStruct((64, 6, LA...]
    pallas_call x1, Pallas kernels: 0.83 us -> 0.33 us  [regroup(): pl.pallas_call(regroup_kernel, out_shape=jax.ShapeDtypeStruct((384, LANES...]
  transfers between devices with their start and end apart: 1 -> 2, of which waited for: 1 -> 1; matrix products, arithmetic and copies ran while one was open for 2% -> 2% of each run, Pallas kernels for 2% -> 2%
where the time goes in v6:
time: 43.1 us; the launch traced here: 42.8 us
  starting transfers between devices  26.1 us (61%)
  blocking collectives  8.51 us (20%)
  Pallas kernels  5.93 us (14%)
  local copies, waits for them, and re-layouts  1.18 us (3%)
  waiting for transfers between devices  0.8 us (2%)
    all_to_all x1, starting transfers between devices, body(): lax.all_to_all(chunks, 'slot', 0, 0, tiled=True, axis_index_groups=[order])  22.9 us
    all_to_all x1, blocking collectives, body(): lax.all_to_all(windows.reshape(8, 48, LANES), ('chan', 'core'), 0, 0, til...  8.51 us
    ppermute x1, starting transfers between devices, body(): other = lax.ppermute(info, 'core', [(0, 1), (1, 0)])  3.15 us
    pallas_call x1, Pallas kernels, compress(): pl.pallas_call(compress_kernel, out_shape=jax.ShapeDtypeStruct((64, 6, LA...  3.11 us
    pallas_call x1, Pallas kernels, azimuth(): pl.pallas_call(azimuth_kernel, out_shape=jax.ShapeDtypeStruct((256, LANES...  1.54 us
    pallas_call x1, Pallas kernels, bands(): pl.pallas_call(bands_kernel, out_shape=(jax.ShapeDtypeStruct((2304, LANES...  0.95 us
  transfers between devices with their start and end apart: 2, of which 1 were waited for; matrix products, arithmetic and copies ran while one was open for 2% of the time, Pallas kernels for 2%

profile of v6, /device:TPU:1, one launch (start us, length us, event | category | flops | bytes accessed | tf_op | source)
XLA Modules:
  0.0 42.8 jit_solution(6656642492023886004)
XLA Ops:
  0.0 3.1 %compress.1 = bf16[64,6,128]{2,1,0:T(8,128)(2,1)} custom-call(bf16[4,4,2,8192]{3,2,1,0:T(2,128)(2,1)} %echo_ref.1, bf16[2,4096]{1,0:T(2,128)(2,1)} %replica_hbm.1), custom_call_target="tpu_custom_call" | custom-call | flops 603979776 | bytes 1048576 | tf_op jit(solution)/shard_map/compress/pallas_call | solution.py:106
  3.1 0.0 copy-start.3
  3.1 22.9 %all-to-all-start = ((bf16[64,6,128]{2,1,0:T(8,128)(2,1)}), bf16[64,6,128]{2,1,0:T(8,128)(2,1)S(1)}, u32[]{:S(2)}, u32[]{:S(2)}) async-start(bf16[64,6,128]{2,1,0:T(8,128)(2,1)} %compress.1), calls=%async_computation | async-start | bytes 262144 | tf_op jit(solution)/shard_map/all_to_all | solution.py:303
  26.1 0.0 copy-done.3
  26.2 0.1 pad_maximum_fusion.1
  26.2 0.3 copy.14
  26.6 0.3 copy.15
  26.8 0.0 copy-start
  26.9 0.0 copy-start.1
  26.9 0.0 copy-start.2
  26.9 0.1 pad_maximum_fusion.filter_ref
  27.0 0.5 %copy-done = s32[2,8]{1,0:T(2,128)S(1)} copy-done((s32[2,8]{1,0:T(2,128)S(1)}, s32[2,8]{1,0:T(2,128)}, u32[]{:S(2)}) %copy-start) | copy-done | bytes 88
  27.5 0.0 copy-done.1
  27.5 0.0 copy-done.2
  27.5 0.9 %bands.1 = (bf16[2304,128]{1,0:T(8,128)(2,1)S(1)}, s32[8,128]{1,0:T(8,128)S(1)}) custom-call(bf16[64,32,32]{2,1,0:T(8,128)(2,1)S(1)} %pad_maximum_fusion.filter_ref, s32[8]{0:T(128)S(1)} %copy-done.1, s32[8]{0:T(128)S(1)} %copy-done.2, s32[2,8]{1,0:T(2,128)S(1)} %copy-done), custom_call_target="tpu_custom_call" | custom-call | flops 1048576 | bytes 1048576 | tf_op jit(solution)/shard_map/bands/pallas_call | solution.py:228
  28.5 3.2 %collective-permute-start = (s32[8,128]{1,0:T(8,128)S(1)}, s32[8,128]{1,0:T(8,128)S(1)}, u32[]{:S(2)}, u32[]{:S(2)}) collective-permute-start(s32[8,128]{1,0:T(8,128)S(1)} %get-tuple-element.15.info_ref), channel_id=1, source_target_pairs={{0,4},{4,0},{1,5},{5,1},{2,6},{6,2},{3,7},{7,3},{8,12},{12,8},{9,1... | collective-permute-start | bytes 12296 | tf_op jit(solution)/shard_map/ppermute | solution.py:310
  31.6 0.8 %collective-permute-done.other_ref = s32[8,128]{1,0:T(8,128)S(1)} collective-permute-done((s32[8,128]{1,0:T(8,128)S(1)}, s32[8,128]{1,0:T(8,128)S(1)}, u32[]{:S(2)}, u32[]{:S(2)}) %collective-permute-start) | collective-permute-done | bytes 4128 | tf_op jit(solution)/shard_map/ppermute | solution.py:310
  32.4 0.0 all-to-all-done.turned_ref
  32.5 0.3 regroup.1
  32.8 8.5 %all_to_all.10 = bf16[8,48,128]{2,1,0:T(8,128)(2,1)S(1)} all-to-all(bf16[8,48,128]{2,1,0:T(8,128)(2,1)S(1)} %bitcast.22), channel_id=1, replica_groups={{6,2,7,3,4,0,5,1},{14,10,15,11,12,8,13,9},{22,18,23,19,20,16,21,17},{30..., dimensions={0} | all-to-all | bytes 196608 | tf_op jit(solution)/shard_map/all_to_all | solution.py:312
  41.3 1.5 %azimuth.1 = bf16[256,128]{1,0:T(8,128)(2,1)} custom-call(bf16[384,128]{1,0:T(8,128)(2,1)S(1)} %bitcast.23, bf16[2304,128]{1,0:T(8,128)(2,1)S(1)} %get-tuple-element.16.bands_ref), custom_call_target="tpu_custom_call" | custom-call | flops 150994944 | bytes 1048576 | tf_op jit(solution)/shard_map/azimuth/pallas_call | solution.py:273
  (5 shorter events, 0.1 us)
Async XLA Ops:
  3.1 23.0 %copy-start.3 = (bf16[16,16,2,64]{3,2,1,0:T(2,128)(2,1)S(1)}, bf16[16,16,2,64]{3,2,1,0:T(2,128)(2,1)}, u32[]{:S(2)}) copy-start(bf16[16,16,2,64]{3,2,1,0:T(2,128)(2,1)} %param.8) | copy-start | bytes 196612
  3.1 29.3 %all-to-all-start = ((bf16[64,6,128]{2,1,0:T(8,128)(2,1)}), bf16[64,6,128]{2,1,0:T(8,128)(2,1)S(1)}, u32[]{:S(2)}, u32[]{:S(2)}) async-start(bf16[64,6,128]{2,1,0:T(8,128)(2,1)} %compress.1), calls=%async_computation | async-start | bytes 262144 | tf_op jit(solution)/shard_map/all_to_all | solution.py:303
  26.8 0.7 %copy-start = (s32[2,8]{1,0:T(2,128)S(1)}, s32[2,8]{1,0:T(2,128)}, u32[]{:S(2)}) copy-start(s32[2,8]{1,0:T(2,128)} %edges_ref) | copy-start | bytes 196
  26.9 0.7 %copy-start.1 = (s32[8]{0:T(128)S(1)}, s32[8]{0:T(128)}, u32[]{:S(2)}) copy-start(s32[8]{0:T(128)} %offset_ref) | copy-start | bytes 100
  26.9 0.7 %copy-start.2 = (s32[8]{0:T(128)S(1)}, s32[8]{0:T(128)}, u32[]{:S(2)}) copy-start(s32[8]{0:T(128)} %width_ref) | copy-start | bytes 100
  28.5 4.0 %collective-permute-start = (s32[8,128]{1,0:T(8,128)S(1)}, s32[8,128]{1,0:T(8,128)S(1)}, u32[]{:S(2)}, u32[]{:S(2)}) collective-permute-start(s32[8,128]{1,0:T(8,128)S(1)} %get-tuple-element.15.info_ref), channel_id=1, source_target_pairs={{0,4},{4,0},{1,5},{5,1},{2,6},{6,2},{3,7},{7,3},{8,12},{12,8},{9,1... | collective-permute-start | bytes 12296 | tf_op jit(solution)/shard_map/ppermute | solution.py:310

commit v7 on v6

--- a/solution.py
+++ b/solution.py
@@ -38,7 +38,7 @@
 
 
 def compress_kernel(
-    echo_ref, replica_hbm, out_ref, replica_ref, echo_rows, sems, taps, windows, parts, rows, chunks
+    echo_ref, replica_hbm, out_ref, replica_ref, echo_rows, sems, taps, windows, parts, rows, chunks, packed
 ):
     taps_copy = pltpu.make_async_copy(replica_hbm, replica_ref, sems.at[16])
     taps_copy.start()
@@ -84,6 +84,7 @@
     for w in range(8):
         windows[32 * w : 32 * w + 32, :] = echo_rows[:, 512 * w : 512 * w + 4608]
     product = lax.dot_general(taps[...], windows[...], NT, preferred_element_type=F32)
+    out_copies = []
     real_lane = lane_ids(128) % 2 == 0
     for half in range(2):
         by_real = product[:128, 128 * half : 128 * half + 128]
@@ -95,11 +96,23 @@
         for w, piece in enumerate(swap_blocks(pieces, 32)):
             at = 128 * half + 32 * w
             rows[at : at + 32, :] = piece
-    rows[256:264, :] = jnp.zeros((8, LANES), F32)
-    for at, slot, count in SEGMENTS:
-        for k in range(6):
-            chunks[at : at + count, k, :] = rows[pl.ds(4 * slot + k, count, stride=4), :]
-    out_ref[...] = chunks[:, 0:6, :].astype(BF16)
+        if half == 0:
+            rows[256:264, :] = jnp.zeros((8, LANES), F32)
+        for at, slot, count in ((64 - FIRST, 0, 24),) if half == 0 else (
+            (0, FIRST, 64 - FIRST),
+            (88 - FIRST, 24, FIRST - 24),
+        ):
+            for k in range(6):
+                chunks[at : at + count, k, :] = rows[pl.ds(4 * slot + k, count, stride=4), :]
+            packed[at : at + count] = chunks[at : at + count, 0:6, :].astype(BF16)
+            out_copies.append(
+                pltpu.make_async_copy(
+                    packed.at[pl.ds(at, count)], out_ref.at[pl.ds(at, count)], sems.at[at // 8]
+                )
+            )
+            out_copies[-1].start()
+    for copy in out_copies:
+        copy.wait()
 
 
 def compress(echoes, replica):
@@ -119,7 +132,9 @@
             pltpu.VMEM((256, LANES), F32),
             pltpu.VMEM((264, LANES), F32),
             pltpu.VMEM((64, 8, LANES), F32),
+            pltpu.VMEM((64, 6, LANES), BF16),
         ],
+        out_specs=pl.BlockSpec(memory_space=pltpu.HBM),
         compiler_params=pltpu.CompilerParams(vmem_limit_bytes=16 << 20),
         cost_estimate=pl.CostEstimate(
             flops=2 * 256 * 256 * 4608, bytes_accessed=1 << 20, transcendentals=0
@@ -251,14 +266,10 @@
     field[384:392, :] = jnp.zeros((8, LANES), F32)
     pair[:, :LANES] = field[0:384, :].astype(BF16)
     pair[:, LANES:] = field[8:392, :].astype(BF16)
-    total = jnp.zeros((256, LANES), F32)
-    for e in range(9):
-        total = total + jnp.dot(
-            pair[16 * e : 16 * e + 256, :],
-            bands_ref[256 * e : 256 * e + 256, :],
-            preferred_element_type=F32,
-        )
-    result[...] = total
+    steps = [pair[16 * e : 16 * e + 256, :] for e in range(9)]
+    result[...] = jnp.dot(
+        jnp.concatenate(steps, axis=1), bands_ref[...], preferred_element_type=F32
+    )
     for half in range(2):
         arrays = [result[pl.ds(4 * half + i, 32, stride=8), :] for i in range(4)]
         for jo, piece in enumerate(swap_blocks(arrays, 32)):

time: 43.1 us -> 43.1 us (level)
  no operation moved by 1% of the time
where the time goes in v7:
time: 43.1 us; the launch traced here: 42.8 us
  starting transfers between devices  26.1 us (61%)
  blocking collectives  8.52 us (20%)
  Pallas kernels  5.9 us (14%)
  local copies, waits for them, and re-layouts  1.18 us (3%)
  waiting for transfers between devices  0.8 us (2%)
    all_to_all x1, starting transfers between devices, body(): lax.all_to_all(chunks, 'slot', 0, 0, tiled=True, axis_index_groups=[order])  22.9 us
    all_to_all x1, blocking collectives, body(): lax.all_to_all(windows.reshape(8, 48, LANES), ('chan', 'core'), 0, 0, til...  8.52 us
    ppermute x1, starting transfers between devices, body(): other = lax.ppermute(info, 'core', [(0, 1), (1, 0)])  3.14 us
    pallas_call x1, Pallas kernels, compress(): pl.pallas_call(compress_kernel, out_shape=jax.ShapeDtypeStruct((64, 6, LA...  3.08 us
    pallas_call x1, Pallas kernels, azimuth(): pl.pallas_call(azimuth_kernel, out_shape=jax.ShapeDtypeStruct((256, LANES...  1.54 us
    pallas_call x1, Pallas kernels, bands(): pl.pallas_call(bands_kernel, out_shape=(jax.ShapeDtypeStruct((2304, LANES...  0.95 us
  transfers between devices with their start and end apart: 2, of which 1 were waited for; matrix products, arithmetic and copies ran while one was open for 2% of the time, Pallas kernels for 2%

profile of v7, /device:TPU:1, one launch (start us, length us, event | category | flops | bytes accessed | tf_op | source)
XLA Modules:
  0.0 42.8 jit_solution(8222591825671984106)
XLA Ops:
  0.0 3.1 %compress.1 = bf16[64,6,128]{2,1,0:T(8,128)(2,1)} custom-call(bf16[4,4,2,8192]{3,2,1,0:T(2,128)(2,1)} %echo_ref.1, bf16[2,4096]{1,0:T(2,128)(2,1)} %replica_hbm.1), custom_call_target="tpu_custom_call" | custom-call | flops 603979776 | bytes 1048576 | tf_op jit(solution)/shard_map/compress/pallas_call | solution.py:119
  3.1 0.0 copy-start.3
  3.1 22.9 %all-to-all-start = ((bf16[64,6,128]{2,1,0:T(8,128)(2,1)}), bf16[64,6,128]{2,1,0:T(8,128)(2,1)S(1)}, u32[]{:S(2)}, u32[]{:S(2)}) async-start(bf16[64,6,128]{2,1,0:T(8,128)(2,1)} %compress.1), calls=%async_computation | async-start | bytes 262144 | tf_op jit(solution)/shard_map/all_to_all | solution.py:314
  26.0 0.0 copy-done.3
  26.1 0.1 pad_maximum_fusion.1
  26.2 0.3 copy.14
  26.5 0.3 copy.15
  26.8 0.0 copy-start
  26.8 0.0 copy-start.1
  26.8 0.0 copy-start.2
  26.8 0.1 pad_maximum_fusion.filter_ref
  27.0 0.5 %copy-done = s32[2,8]{1,0:T(2,128)S(1)} copy-done((s32[2,8]{1,0:T(2,128)S(1)}, s32[2,8]{1,0:T(2,128)}, u32[]{:S(2)}) %copy-start) | copy-done | bytes 88
  27.5 0.0 copy-done.1
  27.5 0.0 copy-done.2
  27.5 1.0 %bands.1 = (bf16[2304,128]{1,0:T(8,128)(2,1)S(1)}, s32[8,128]{1,0:T(8,128)S(1)}) custom-call(bf16[64,32,32]{2,1,0:T(8,128)(2,1)S(1)} %pad_maximum_fusion.filter_ref, s32[8]{0:T(128)S(1)} %copy-done.1, s32[8]{0:T(128)S(1)} %copy-done.2, s32[2,8]{1,0:T(2,128)S(1)} %copy-done), custom_call_target="tpu_custom_call" | custom-call | flops 1048576 | bytes 1048576 | tf_op jit(solution)/shard_map/bands/pallas_call | solution.py:243
  28.5 3.1 %collective-permute-start = (s32[8,128]{1,0:T(8,128)S(1)}, s32[8,128]{1,0:T(8,128)S(1)}, u32[]{:S(2)}, u32[]{:S(2)}) collective-permute-start(s32[8,128]{1,0:T(8,128)S(1)} %get-tuple-element.15.info_ref), channel_id=1, source_target_pairs={{0,4},{4,0},{1,5},{5,1},{2,6},{6,2},{3,7},{7,3},{8,12},{12,8},{9,1... | collective-permute-start | bytes 12296 | tf_op jit(solution)/shard_map/ppermute | solution.py:321
  31.6 0.8 %collective-permute-done.other_ref = s32[8,128]{1,0:T(8,128)S(1)} collective-permute-done((s32[8,128]{1,0:T(8,128)S(1)}, s32[8,128]{1,0:T(8,128)S(1)}, u32[]{:S(2)}, u32[]{:S(2)}) %collective-permute-start) | collective-permute-done | bytes 4128 | tf_op jit(solution)/shard_map/ppermute | solution.py:321
  32.4 0.0 all-to-all-done.turned_ref
  32.4 0.3 regroup.1
  32.7 8.5 %all_to_all.10 = bf16[8,48,128]{2,1,0:T(8,128)(2,1)S(1)} all-to-all(bf16[8,48,128]{2,1,0:T(8,128)(2,1)S(1)} %bitcast.22), channel_id=1, replica_groups={{6,2,7,3,4,0,5,1},{14,10,15,11,12,8,13,9},{22,18,23,19,20,16,21,17},{30..., dimensions={0} | all-to-all | bytes 196608 | tf_op jit(solution)/shard_map/all_to_all | solution.py:323
  41.3 1.5 %azimuth.1 = bf16[256,128]{1,0:T(8,128)(2,1)} custom-call(bf16[384,128]{1,0:T(8,128)(2,1)S(1)} %bitcast.23, bf16[2304,128]{1,0:T(8,128)(2,1)S(1)} %get-tuple-element.16.bands_ref), custom_call_target="tpu_custom_call" | custom-call | flops 150994944 | bytes 1048576 | tf_op jit(solution)/shard_map/azimuth/pallas_call | solution.py:284
  (5 shorter events, 0.1 us)
Async XLA Ops:
  3.1 23.0 %copy-start.3 = (bf16[16,16,2,64]{3,2,1,0:T(2,128)(2,1)S(1)}, bf16[16,16,2,64]{3,2,1,0:T(2,128)(2,1)}, u32[]{:S(2)}) copy-start(bf16[16,16,2,64]{3,2,1,0:T(2,128)(2,1)} %param.8) | copy-start | bytes 196612
  3.1 29.3 %all-to-all-start = ((bf16[64,6,128]{2,1,0:T(8,128)(2,1)}), bf16[64,6,128]{2,1,0:T(8,128)(2,1)S(1)}, u32[]{:S(2)}, u32[]{:S(2)}) async-start(bf16[64,6,128]{2,1,0:T(8,128)(2,1)} %compress.1), calls=%async_computation | async-start | bytes 262144 | tf_op jit(solution)/shard_map/all_to_all | solution.py:314
  26.8 0.7 %copy-start = (s32[2,8]{1,0:T(2,128)S(1)}, s32[2,8]{1,0:T(2,128)}, u32[]{:S(2)}) copy-start(s32[2,8]{1,0:T(2,128)} %edges_ref) | copy-start | bytes 196
  26.8 0.7 %copy-start.1 = (s32[8]{0:T(128)S(1)}, s32[8]{0:T(128)}, u32[]{:S(2)}) copy-start(s32[8]{0:T(128)} %offset_ref) | copy-start | bytes 100
  26.8 0.7 %copy-start.2 = (s32[8]{0:T(128)S(1)}, s32[8]{0:T(128)}, u32[]{:S(2)}) copy-start(s32[8]{0:T(128)} %width_ref) | copy-start | bytes 100
  28.5 3.9 %collective-permute-start = (s32[8,128]{1,0:T(8,128)S(1)}, s32[8,128]{1,0:T(8,128)S(1)}, u32[]{:S(2)}, u32[]{:S(2)}) collective-permute-start(s32[8,128]{1,0:T(8,128)S(1)} %get-tuple-element.15.info_ref), channel_id=1, source_target_pairs={{0,4},{4,0},{1,5},{5,1},{2,6},{6,2},{3,7},{7,3},{8,12},{12,8},{9,1... | collective-permute-start | bytes 12296 | tf_op jit(solution)/shard_map/ppermute | solution.py:321

commit v8 on v7

--- a/solution.py
+++ b/solution.py
@@ -11,7 +11,7 @@
 LANES = 128
 NT = (((1,), (1,)), ((), ()))
 FIRST = 40
-LAST = ((2, 1), (2, 0), (3, 1), (3, 0), (0, 1), (0, 0), (1, 1), (1, 0))
+LAST = ((2, 1), (3, 1), (0, 1), (1, 1), (2, 0), (3, 0), (0, 0), (1, 0))
 SEGMENTS = ((0, FIRST, 64 - FIRST), (64 - FIRST, 0, FIRST))
 
 
@@ -266,9 +266,9 @@
     field[384:392, :] = jnp.zeros((8, LANES), F32)
     pair[:, :LANES] = field[0:384, :].astype(BF16)
     pair[:, LANES:] = field[8:392, :].astype(BF16)
-    steps = [pair[16 * e : 16 * e + 256, :] for e in range(9)]
+    steps = [pair[16 * e : 16 * e + 256, :] for e in range(8)] + [pair[128:384, :LANES]]
     result[...] = jnp.dot(
-        jnp.concatenate(steps, axis=1), bands_ref[...], preferred_element_type=F32
+        jnp.concatenate(steps, axis=1), bands_ref[0:2176, :], preferred_element_type=F32
     )
     for half in range(2):
         arrays = [result[pl.ds(4 * half + i, 32, stride=8), :] for i in range(4)]

time: 43.1 us -> 42.8 us (level)
  no operation moved by 1% of the time
where the time goes in v8:
time: 42.8 us; the launch traced here: 42.5 us
  starting transfers between devices  26.1 us (61%)
  blocking collectives  8.26 us (19%)
  Pallas kernels  5.88 us (14%)
  local copies, waits for them, and re-layouts  1.18 us (3%)
  waiting for transfers between devices  0.8 us (2%)
    all_to_all x1, starting transfers between devices, body(): lax.all_to_all(chunks, 'slot', 0, 0, tiled=True, axis_index_groups=[order])  22.9 us
    all_to_all x1, blocking collectives, body(): lax.all_to_all(windows.reshape(8, 48, LANES), ('chan', 'core'), 0, 0, til...  8.26 us
    ppermute x1, starting transfers between devices, body(): other = lax.ppermute(info, 'core', [(0, 1), (1, 0)])  3.14 us
    pallas_call x1, Pallas kernels, compress(): pl.pallas_call(compress_kernel, out_shape=jax.ShapeDtypeStruct((64, 6, LA...  3.08 us
    pallas_call x1, Pallas kernels, azimuth(): pl.pallas_call(azimuth_kernel, out_shape=jax.ShapeDtypeStruct((256, LANES...  1.53 us
    pallas_call x1, Pallas kernels, bands(): pl.pallas_call(bands_kernel, out_shape=(jax.ShapeDtypeStruct((2304, LANES...  0.95 us
  transfers between devices with their start and end apart: 2, of which 1 were waited for; matrix products, arithmetic and copies ran while one was open for 2% of the time, Pallas kernels for 2%

profile of v8, /device:TPU:1, one launch (start us, length us, event | category | flops | bytes accessed | tf_op | source)
XLA Modules:
  0.0 42.5 jit_solution(3906613751573208648)
XLA Ops:
  0.0 3.1 %compress.1 = bf16[64,6,128]{2,1,0:T(8,128)(2,1)} custom-call(bf16[4,4,2,8192]{3,2,1,0:T(2,128)(2,1)} %echo_ref.1, bf16[2,4096]{1,0:T(2,128)(2,1)} %replica_hbm.1), custom_call_target="tpu_custom_call" | custom-call | flops 603979776 | bytes 1048576 | tf_op jit(solution)/shard_map/compress/pallas_call | solution.py:119
  3.1 0.0 copy-start.3
  3.1 22.9 %all-to-all-start = ((bf16[64,6,128]{2,1,0:T(8,128)(2,1)}), bf16[64,6,128]{2,1,0:T(8,128)(2,1)S(1)}, u32[]{:S(2)}, u32[]{:S(2)}) async-start(bf16[64,6,128]{2,1,0:T(8,128)(2,1)} %compress.1), calls=%async_computation | async-start | bytes 262144 | tf_op jit(solution)/shard_map/all_to_all | solution.py:314
  26.0 0.0 copy-done.3
  26.1 0.1 pad_maximum_fusion.1
  26.2 0.3 copy.14
  26.5 0.3 copy.15
  26.8 0.0 copy-start
  26.8 0.0 copy-start.1
  26.8 0.0 copy-start.2
  26.8 0.1 pad_maximum_fusion.filter_ref
  27.0 0.5 %copy-done = s32[2,8]{1,0:T(2,128)S(1)} copy-done((s32[2,8]{1,0:T(2,128)S(1)}, s32[2,8]{1,0:T(2,128)}, u32[]{:S(2)}) %copy-start) | copy-done | bytes 88
  27.5 0.0 copy-done.1
  27.5 0.0 copy-done.2
  27.5 1.0 %bands.1 = (bf16[2304,128]{1,0:T(8,128)(2,1)S(1)}, s32[8,128]{1,0:T(8,128)S(1)}) custom-call(bf16[64,32,32]{2,1,0:T(8,128)(2,1)S(1)} %pad_maximum_fusion.filter_ref, s32[8]{0:T(128)S(1)} %copy-done.1, s32[8]{0:T(128)S(1)} %copy-done.2, s32[2,8]{1,0:T(2,128)S(1)} %copy-done), custom_call_target="tpu_custom_call" | custom-call | flops 1048576 | bytes 1048576 | tf_op jit(solution)/shard_map/bands/pallas_call | solution.py:243
  28.5 3.1 %collective-permute-start = (s32[8,128]{1,0:T(8,128)S(1)}, s32[8,128]{1,0:T(8,128)S(1)}, u32[]{:S(2)}, u32[]{:S(2)}) collective-permute-start(s32[8,128]{1,0:T(8,128)S(1)} %get-tuple-element.15.info_ref), channel_id=1, source_target_pairs={{0,4},{4,0},{1,5},{5,1},{2,6},{6,2},{3,7},{7,3},{8,12},{12,8},{9,1... | collective-permute-start | bytes 12296 | tf_op jit(solution)/shard_map/ppermute | solution.py:321
  31.6 0.8 %collective-permute-done.other_ref = s32[8,128]{1,0:T(8,128)S(1)} collective-permute-done((s32[8,128]{1,0:T(8,128)S(1)}, s32[8,128]{1,0:T(8,128)S(1)}, u32[]{:S(2)}, u32[]{:S(2)}) %collective-permute-start) | collective-permute-done | bytes 4128 | tf_op jit(solution)/shard_map/ppermute | solution.py:321
  32.4 0.0 all-to-all-done.turned_ref
  32.4 0.3 regroup.1
  32.7 8.3 %all_to_all.10 = bf16[8,48,128]{2,1,0:T(8,128)(2,1)S(1)} all-to-all(bf16[8,48,128]{2,1,0:T(8,128)(2,1)S(1)} %bitcast.22), channel_id=1, replica_groups={{6,7,4,5,2,3,0,1},{14,15,12,13,10,11,8,9},{22,23,20,21,18,19,16,17},{30..., dimensions={0} | all-to-all | bytes 196608 | tf_op jit(solution)/shard_map/all_to_all | solution.py:323
  41.0 1.5 %azimuth.1 = bf16[256,128]{1,0:T(8,128)(2,1)} custom-call(bf16[384,128]{1,0:T(8,128)(2,1)S(1)} %bitcast.23, bf16[2304,128]{1,0:T(8,128)(2,1)S(1)} %get-tuple-element.16.bands_ref), custom_call_target="tpu_custom_call" | custom-call | flops 150994944 | bytes 1048576 | tf_op jit(solution)/shard_map/azimuth/pallas_call | solution.py:284
  (5 shorter events, 0.1 us)
Async XLA Ops:
  3.1 23.0 %copy-start.3 = (bf16[16,16,2,64]{3,2,1,0:T(2,128)(2,1)S(1)}, bf16[16,16,2,64]{3,2,1,0:T(2,128)(2,1)}, u32[]{:S(2)}) copy-start(bf16[16,16,2,64]{3,2,1,0:T(2,128)(2,1)} %param.8) | copy-start | bytes 196612
  3.1 29.3 %all-to-all-start = ((bf16[64,6,128]{2,1,0:T(8,128)(2,1)}), bf16[64,6,128]{2,1,0:T(8,128)(2,1)S(1)}, u32[]{:S(2)}, u32[]{:S(2)}) async-start(bf16[64,6,128]{2,1,0:T(8,128)(2,1)} %compress.1), calls=%async_computation | async-start | bytes 262144 | tf_op jit(solution)/shard_map/all_to_all | solution.py:314
  26.8 0.7 %copy-start = (s32[2,8]{1,0:T(2,128)S(1)}, s32[2,8]{1,0:T(2,128)}, u32[]{:S(2)}) copy-start(s32[2,8]{1,0:T(2,128)} %edges_ref) | copy-start | bytes 196
  26.8 0.7 %copy-start.1 = (s32[8]{0:T(128)S(1)}, s32[8]{0:T(128)}, u32[]{:S(2)}) copy-start(s32[8]{0:T(128)} %offset_ref) | copy-start | bytes 100
  26.8 0.7 %copy-start.2 = (s32[8]{0:T(128)S(1)}, s32[8]{0:T(128)}, u32[]{:S(2)}) copy-start(s32[8]{0:T(128)} %width_ref) | copy-start | bytes 100
  28.5 3.9 %collective-permute-start = (s32[8,128]{1,0:T(8,128)S(1)}, s32[8,128]{1,0:T(8,128)S(1)}, u32[]{:S(2)}, u32[]{:S(2)}) collective-permute-start(s32[8,128]{1,0:T(8,128)S(1)} %get-tuple-element.15.info_ref), channel_id=1, source_target_pairs={{0,4},{4,0},{1,5},{5,1},{2,6},{6,2},{3,7},{7,3},{8,12},{12,8},{9,1... | collective-permute-start | bytes 12296 | tf_op jit(solution)/shard_map/ppermute | solution.py:321
